TPU v7x, 512 devices: a whole 4x4x16 slice. The times are simulated.
512 devices in a mesh: ctx: 64 (over z_hi, x, y), exp: 8 (over z_lo, core).
Axes of the slice: x: 4, y: 4, z: 16 (z_hi: 4, z_lo: 4; z = z_hi * 4 + z_lo), core: 2. Of those that a mesh axis runs over, the one named last changes fastest.
Arguments:
- queries: bfloat16 [65536, 2048], P('ctx', 'exp'), may hold values from -150 to 150
- keys: bfloat16 [65536, 2048], P('ctx', 'exp'), may hold values from -6 to 6
- values: bfloat16 [65536, 2048], P('ctx', 'exp'), may hold values from -6 to 6
- segment_ids: int32 [65536], P('ctx'), may hold values from 0 to 255, never falling along the last dimension, each value on 1 to 1024 neighbouring positions
- out_proj: bfloat16 [2048, 1280], P('exp'), may hold values from -0.125 to 0.125
- residual: bfloat16 [65536, 1280], P(('ctx', 'exp')), may hold values from -6 to 6
- norm_gain: float32 [1280], replicated, may hold values from 0.1 to 1.9
- expert_ids: int32 [65536, 6], P(('ctx', 'exp')), may hold values from 0 to 63, all different within a row; in each aligned block of 128 rows (0 to 127, 128 to 255, ...) at most 16 rows name the same one
- gate_weights: float32 [65536, 6], P(('ctx', 'exp')), may hold values from 0.05 to 0.4
- expert_up: bfloat16 [64, 768, 1280], P('ctx', 'exp'), may hold values from -0.15625 to 0.15625
- expert_down: bfloat16 [64, 768, 1280], P('ctx', 'exp'), may hold values from -0.21875 to 0.21875
Outputs:
- layer_out: bfloat16 [65536, 1280], P(('ctx', 'exp'))
Inputs may be any that keep to these rules, and one draw needn't show every extreme that they name: `segment_ids`: segment ids never fall; every segment spans 1 to 1024 consecutive tokens, one exactly 1024. `expert_ids`: each row names 6 different experts. In each aligned block of 128 rows (the rows of one device) no expert is named by more than 16 rows, a bound that some block reaches.
All inputs are finite; a program needn't handle non-finite values.
Results may differ from a plain program's by a relative error of at most 0.01.
Values may be sent and summed in bfloat16 or wider, within the bound.
A program may use at most 64 MiB of HBM per device.

v0:
```python
import jax
import jax.numpy as jnp
from jax import lax
from jax.sharding import PartitionSpec as P

HEAD = 128
TOP = 6


def shifted(block, axis, distance):
    devices = range(lax.axis_size(axis))
    route = [(i - distance, i) for i in devices if i - distance in devices]
    return lax.ppermute(block, axis, route)


def block_attention(query_rows, key_rows, value_rows, allowed):
    scores = jnp.dot(query_rows, key_rows.T, preferred_element_type=jnp.float32) * HEAD ** (-0.5)
    row_max = jnp.max(jnp.where(allowed, scores, -1e30), axis=1, keepdims=True)
    weights = jnp.exp(jnp.where(allowed, scores - row_max, -jnp.inf))
    probabilities = (weights / jnp.sum(weights, axis=1, keepdims=True)).astype(jnp.bfloat16)
    return jnp.dot(probabilities, value_rows, preferred_element_type=jnp.float32).astype(
        jnp.bfloat16
    )


def shards(
    queries,
    keys,
    values,
    segment_ids,
    out_proj,
    residual,
    norm_gain,
    expert_ids,
    gate_weights,
    expert_up,
    expert_down,
):
    up_whole, down_whole = (
        lax.all_gather(expert_up, "exp", axis=1, tiled=True),
        lax.all_gather(expert_down, "exp", axis=1, tiled=True),
    )
    shard_len = queries.shape[0]
    heads_here = queries.shape[1] // HEAD
    block_rows = min(512, shard_len)
    blocks = shard_len // block_rows
    seg_marks = segment_ids + 1
    early_keys, early_values, early_marks = shifted((keys, values, seg_marks), "ctx", 1)
    positions = jnp.arange(shard_len, dtype=jnp.int32)
    both_marks = jnp.concatenate([early_marks, seg_marks])
    both_positions = jnp.concatenate([positions - shard_len, positions])
    head_outputs = []
    for head_index in range(heads_here):
        low = head_index * HEAD
        query_head = queries[:, low : low + HEAD]
        key_head = keys[:, low : low + HEAD]
        value_head = values[:, low : low + HEAD]
        both_keys = jnp.concatenate([early_keys[:, low : low + HEAD], key_head], axis=0)
        both_values = jnp.concatenate([early_values[:, low : low + HEAD], value_head], axis=0)

        def one_block(block_index):
            start_row = block_index * block_rows
            query_rows = lax.dynamic_slice_in_dim(query_head, start_row, block_rows, 0)
            query_marks = lax.dynamic_slice_in_dim(seg_marks, start_row, block_rows, 0)
            query_positions = start_row + jnp.arange(block_rows, dtype=jnp.int32)
            allowed = (both_marks[None, :] == query_marks[:, None]) & (
                both_positions[None, :] <= query_positions[:, None]
            )
            return block_attention(query_rows, both_keys, both_values, allowed)

        block_outputs = lax.map(one_block, jnp.arange(blocks, dtype=jnp.int32))
        head_outputs.append(block_outputs.reshape(shard_len, HEAD))
    attention = jnp.concatenate(head_outputs, axis=1)
    row_block = attention
    projected = lax.psum_scatter(
        jnp.dot(row_block, out_proj, preferred_element_type=jnp.float32).astype(jnp.bfloat16),
        "exp",
        scatter_dimension=0,
        tiled=True,
    ).astype(jnp.float32)
    stream = (residual.astype(jnp.float32) + projected).astype(jnp.bfloat16)
    stream_f = stream.astype(jnp.float32)
    mean_square = jnp.mean(stream_f * stream_f, axis=1, keepdims=True)
    normed = (stream_f * lax.rsqrt(mean_square + 1e-06) * norm_gain[None, :]).astype(jnp.bfloat16)
    tok_rows = stream.shape[0]
    feature_count = stream.shape[1]
    experts = lax.axis_size("ctx")
    slot_count = max(2, tok_rows * TOP * 4 // (3 * experts))
    flat_ids = expert_ids.reshape(-1)
    one_hot = (flat_ids[:, None] == jnp.arange(experts, dtype=jnp.int32)[None, :]).astype(jnp.int32)
    earlier = jnp.cumsum(one_hot, axis=0) - one_hot
    slot_rank = jnp.sum(earlier * one_hot, axis=1)
    slot_index = flat_ids * slot_count + slot_rank
    slot_grid = slot_index.reshape(tok_rows, TOP)
    placing = jnp.any(
        slot_grid[None, :, :] == jnp.arange(experts * slot_count, dtype=jnp.int32)[:, None, None],
        axis=2,
    )
    outgoing = jnp.dot(
        placing.astype(jnp.bfloat16), normed, preferred_element_type=jnp.float32
    ).astype(jnp.bfloat16)
    outgoing = outgoing.reshape(experts, slot_count, feature_count)
    arrived = lax.all_to_all(outgoing, "ctx", split_axis=0, concat_axis=0, tiled=True)
    sources, item_count, width_here = arrived.shape
    row_block = arrived.reshape(sources * item_count, width_here)
    hidden = jax.nn.silu(
        jnp.dot(row_block, up_whole[0].T, preferred_element_type=jnp.float32)
    ).astype(jnp.bfloat16)
    result = jnp.dot(hidden, down_whole[0], preferred_element_type=jnp.float32).astype(jnp.bfloat16)
    result = result.reshape(sources, item_count, width_here)
    returned = lax.all_to_all(result, "ctx", split_axis=0, concat_axis=0, tiled=True)
    returned_flat = returned.reshape(experts * slot_count, feature_count)
    picked = returned_flat[slot_index].reshape(tok_rows, TOP, feature_count).astype(jnp.float32)
    mixture = jnp.sum(gate_weights[:, :, None] * picked, axis=1)
    return (stream_f + mixture).astype(jnp.bfloat16)


def solution(mesh):
    in_specs = (
        P("ctx", "exp"),
        P("ctx", "exp"),
        P("ctx", "exp"),
        P("ctx"),
        P("exp", None),
        P(("ctx", "exp"), None),
        P(),
        P(("ctx", "exp"), None),
        P(("ctx", "exp"), None),
        P("ctx", "exp", None),
        P("ctx", "exp", None),
    )
    out_specs = P(("ctx", "exp"), None)
    return jax.shard_map(shards, mesh=mesh, in_specs=in_specs, out_specs=out_specs, check_vma=False)
```

profile of v0, /device:TPU:1, one launch (start us, length us, event | category | flops | bytes accessed | tf_op | source)
XLA Modules:
  0.0 555.1 jit_solution(545644793723613808)
XLA Ops:
  6.5 0.8 broadcast_add_fusion
  7.3 4.0 collective-permute-start
  11.3 3.2 collective-permute-start.1
  14.6 2.9 collective-permute-start.2
  17.5 1.1 fusion.49
  18.5 1.1 fusion.47
  19.6 1.8 fusion.50
  21.4 2.9 collective-permute-done.1
  24.4 11.1 %collective-permute-done.2 = bf16[1024,256]{1,0:T(8,128)(2,1)S(1)} collective-permute-done((bf16[1024,256]{1,0:T(8,128)(2,1)}, bf16[1024,256]{1,0:T(8,128)(2,1)S(1)}, u32[]{:S(2)}, u32[]{:S(2)}) %collective-permute-start.2) | collective-permute-done | bytes 524320 | tf_op jit(solution)/shard_map/ppermute | solution.py:13
  35.6 0.9 pad_maximum_fusion.1
  36.5 15.9 %while.20 = (s32[]{:T(128)}, bf16[2,512,128]{2,1,0:T(8,128)(2,1)S(1)}, s32[2048]{0:T(1024)S(1)}, s32[2]{0:T(128)S(1)}, s32[1024]{0:T(1024)}, /*index=5*/s32[2048...) while((s32[]{:T(128)}, ...), condition=%wide.region_3.4_spmd, body=%wide.region_0.3_spmd.sunk | while | flops 558956032 | bytes 16068835 | solution.py:71
  36.5 0.6 dynamic_slice.34
  37.7 0.8 dynamic_slice.35
  38.5 2.3 select_reduce_fusion.4
  40.7 1.7 fusion.68
  42.4 2.0 fusion.69
  44.4 0.6 dynamic_slice.34
  45.6 0.8 dynamic_slice.35
  46.4 2.2 select_reduce_fusion.4
  48.7 1.7 fusion.68
  50.4 2.0 fusion.69
  52.4 13.9 %while.21 = (s32[]{:T(128)}, bf16[2,512,128]{2,1,0:T(8,128)(2,1)S(1)}, s32[2048]{0:T(1024)S(1)}, s32[2]{0:T(128)S(1)}, s32[1024]{0:T(1024)}, /*index=5*/s32[2048...) while((s32[]{:T(128)}, ...), condition=%wide.region_7.8_spmd, body=%wide.region_4.7_spmd.sunk | while | flops 558956032 | bytes 13971655 | solution.py:71
  52.4 0.6 dynamic_slice.37
  53.7 0.8 dynamic_slice.38
  54.4 1.3 select_reduce_fusion.5
  55.7 1.7 fusion.72
  57.4 2.0 fusion.73
  59.4 0.6 dynamic_slice.37
  60.6 0.8 dynamic_slice.38
  61.4 1.3 select_reduce_fusion.5
  62.7 1.7 fusion.72
  64.4 2.0 fusion.73
  66.4 2.4 convolution_convert_fusion.2
  69.2 1.8 reduce-window.6
  72.2 120.0 %reduce-scatter.2.cloned.1.call-done = bf16[128,1280]{1,0:T(8,128)(2,1)} async-done(((bf16[1024,1280]{1,0:T(8,128)(2,1)}), bf16[128,1280]{1,0:T(8,128)(2,1)}) %reduce-scatter.2.cloned.1.call-update) | async-done | bytes 327696 | tf_op jit(solution)/shard_map/reduce_scatter | solution.py:75
  192.2 1.2 fusion.28
  193.4 3.4 convolution_convert_fusion.1
  196.8 16.9 %all-to-all-start = ((bf16[64,16,1280]{2,1,0:T(8,128)(2,1)}), bf16[64,16,1280]{2,1,0:T(8,128)(2,1)S(1)}, u32[]{:S(2)}, u32[]{:S(2)}) async-start(bf16[64,16,1280]{2,1,0:T(8,128)(2,1)} %bitcast.7), calls=%async_computation.1 | async-start | bytes 5242880 | tf_op jit(solution)/shard_map/all_to_all | solution.py:103
  213.7 0.7 all-gather.3.cloned.1.call-update
  215.2 110.1 %all-gather.3.cloned.1.call-done = bf16[1,768,1280]{2,1,0:T(8,128)(2,1)} async-done(((bf16[1,96,1280]{2,1,0:T(8,128)(2,1)}), bf16[1,768,1280]{2,1,0:T(8,128)(2,1)}) %all-gather.3.cloned.1.call-update) | async-done | bytes 1966096 | tf_op jit(solution)/shard_map/all_gather | solution.py:40
  325.3 63.2 %all-gather.5.cloned.1.call-done = bf16[1,768,1280]{2,1,0:T(8,128)(2,1)} async-done(((bf16[1,96,1280]{2,1,0:T(8,128)(2,1)}), bf16[1,768,1280]{2,1,0:T(8,128)(2,1)}) %all-gather.5.cloned.1.call-update) | async-done | bytes 1966096 | tf_op jit(solution)/shard_map/all_gather | solution.py:41
  388.5 8.0 %convolution_convert_fusion = bf16[1024,1280]{1,0:T(8,128)(2,1)} fusion(bf16[1,768,1280]{2,1,0:T(8,128)(2,1)} %all-gather.5.cloned.1.call-done, bf16[1024,1280]{1,0:T(8,128)(2,1)S(1)} %bitcast.70, bf16[1,768,1280]{2,1,0:T(8,128)(2,1)} %all-gather.3.cloned.1.call-done), kind=kOutput, calls=%fused_computation.32 | convolution fusion | flops 4031774720 | bytes 9175040 | tf_op jit(solution)/shard_map/dot_general | solution.py:109
  396.5 16.2 %all-to-all-start.1 = ((bf16[64,16,1280]{2,1,0:T(8,128)(2,1)}), bf16[64,16,1280]{2,1,0:T(8,128)(2,1)S(1)}, u32[]{:S(2)}, u32[]{:S(2)}) async-start(bf16[64,16,1280]{2,1,0:T(8,128)(2,1)} %bitcast.71), calls=%async_computation.2 | async-start | bytes 5242880 | tf_op jit(solution)/shard_map/all_to_all | solution.py:111
  413.0 122.3 %all-to-all-done.1 = bf16[64,16,1280]{2,1,0:T(8,128)(2,1)S(1)} async-done(((bf16[64,16,1280]{2,1,0:T(8,128)(2,1)}), bf16[64,16,1280]{2,1,0:T(8,128)(2,1)S(1)}, u32[]{:S(2)}, u32[]{:S(2)}) %all-to-all-start.1) | async-done | bytes 2621472 | tf_op jit(solution)/shard_map/all_to_all | solution.py:111
  535.3 3.7 gather_fusion
  539.0 4.5 reshape.112
  543.5 4.2 multiply_reduce_fusion
  547.7 0.8 fusion.31
  (58 shorter events, 2.9 us)
Async XLA Ops:
  6.5 59.8 %copy-start = (bf16[256,1280]{1,0:T(8,128)(2,1)S(1)}, bf16[256,1280]{1,0:T(8,128)(2,1)}, u32[]{:S(2)}) copy-start(bf16[256,1280]{1,0:T(8,128)(2,1)} %param.19) | copy-start | bytes 1966084
  6.5 185.7 %reduce-scatter.2.cloned.1.call-start = ((), (), s32[]{:S(2)}) async-start(), calls=%async_computation.3 | async-start | bytes 2949120 | tf_op jit(solution)/shard_map/reduce_scatter | solution.py:75
  7.3 17.0 %copy-start.5 = (s32[1024]{0:T(1024)}, s32[1024]{0:T(1024)S(1)}, u32[]{:S(2)}) copy-start(s32[1024]{0:T(1024)S(1)} %broadcast_add_fusion) | copy-start | bytes 12292
  7.3 14.1 %collective-permute-start = (s32[1024]{0:T(1024)S(1)}, s32[1024]{0:T(1024)S(1)}, u32[]{:S(2)}, u32[]{:S(2)}) collective-permute-start(s32[1024]{0:T(1024)S(1)} %broadcast_add_fusion), channel_id=1, source_target_pairs={{0,8},{8,16},{16,24},{24,32},{32,40},{40,48},{48,56},{56,64},{64,7... | collective-permute-start | bytes 12296 | tf_op jit(solution)/shard_map/ppermute | solution.py:13
  11.3 13.0 %collective-permute-start.1 = (bf16[1024,256]{1,0:T(8,128)(2,1)}, bf16[1024,256]{1,0:T(8,128)(2,1)S(1)}, u32[]{:S(2)}, u32[]{:S(2)}) collective-permute-start(bf16[1024,256]{1,0:T(8,128)(2,1)} %param.16), channel_id=1, source_target_pairs={{0,8},{8,16},{16,24},{24,32},{32,40},{40,48},{48,56},{56,64},{64,7... | collective-permute-start | bytes 1572872 | tf_op jit(solution)/shard_map/ppermute | solution.py:13
  14.6 21.0 %collective-permute-start.2 = (bf16[1024,256]{1,0:T(8,128)(2,1)}, bf16[1024,256]{1,0:T(8,128)(2,1)S(1)}, u32[]{:S(2)}, u32[]{:S(2)}) collective-permute-start(bf16[1024,256]{1,0:T(8,128)(2,1)} %param.17), channel_id=1, source_target_pairs={{0,8},{8,16},{16,24},{24,32},{32,40},{40,48},{48,56},{56,64},{64,7... | collective-permute-start | bytes 1572872 | tf_op jit(solution)/shard_map/ppermute | solution.py:13
  38.5 4.0 copy-start.4
  46.4 3.9 copy-start.4
  66.4 2.4 copy-start.7
  66.4 125.9 %copy-start.1 = (bf16[128,1280]{1,0:T(8,128)(2,1)S(1)}, bf16[128,1280]{1,0:T(8,128)(2,1)}, u32[]{:S(2)}) copy-start(bf16[128,1280]{1,0:T(8,128)(2,1)} %param.20) | copy-start | bytes 983044
  66.4 127.0 %copy-start.6 = (f32[1280]{0:T(1024)S(1)}, f32[1280]{0:T(1024)}, u32[]{:S(2)}) copy-start(f32[1280]{0:T(1024)} %param.21) | copy-start | bytes 15364
  196.8 191.7 %all-to-all-start = ((bf16[64,16,1280]{2,1,0:T(8,128)(2,1)}), bf16[64,16,1280]{2,1,0:T(8,128)(2,1)S(1)}, u32[]{:S(2)}, u32[]{:S(2)}) async-start(bf16[64,16,1280]{2,1,0:T(8,128)(2,1)} %bitcast.7), calls=%async_computation.1 | async-start | bytes 5242880 | tf_op jit(solution)/shard_map/all_to_all | solution.py:103
  213.7 111.6 %all-gather.3.cloned.1.call-start = ((), (), s32[]{:S(2)}) async-start(), calls=%async_computation.4 | async-start | bytes 2211840 | tf_op jit(solution)/shard_map/all_gather | solution.py:40
  214.4 174.0 %all-gather.5.cloned.1.call-start = ((), (), s32[]{:S(2)}) async-start(), calls=%async_computation.5 | async-start | bytes 2211840 | tf_op jit(solution)/shard_map/all_gather | solution.py:41
  396.5 16.3 %copy-start.8 = (f32[128,6]{0,1:T(8,128)S(1)}, f32[128,6]{0,1:T(8,128)}, u32[]{:S(2)}) copy-start(f32[128,6]{0,1:T(8,128)} %param.23) | copy-start | bytes 9220
  396.5 138.8 %all-to-all-start.1 = ((bf16[64,16,1280]{2,1,0:T(8,128)(2,1)}), bf16[64,16,1280]{2,1,0:T(8,128)(2,1)S(1)}, u32[]{:S(2)}, u32[]{:S(2)}) async-start(bf16[64,16,1280]{2,1,0:T(8,128)(2,1)} %bitcast.71), calls=%async_computation.2 | async-start | bytes 5242880 | tf_op jit(solution)/shard_map/all_to_all | solution.py:111
  543.5 4.2 copy-start.2
  543.5 4.2 copy-start.3
Sparse Core Ops, SparseCore 0:
  68.9 123.2 reduce-scatter.1
  216.6 108.6 all-gather.2
  327.4 61.0 all-gather.4
where the time goes:
time: 557 us; the launch traced here: 555 us
  waiting for transfers between devices  431 us (77%)
  starting transfers between devices  43.5 us (8%)
  matrix products  28.7 us (5%)
  local copies, waits for them, and re-layouts  18.8 us (3%)
  other arithmetic  17.2 us (3%)
  between operations  13.4 us (2%)
    all_to_all x1, waiting for transfers between devices, shards(): lax.all_to_all(result, 'ctx', split_axis=0, concat_axis=0, tiled=True)  122 us
    reduce_scatter x1, waiting for transfers between devices, shards(): lax.psum_scatter(jnp.dot(row_block, out_proj, preferred_element_type=jnp....  120 us
    all_gather x1, waiting for transfers between devices, shards(): lax.all_gather(expert_up, 'exp', axis=1, tiled=True)  110 us
    all_gather x1, waiting for transfers between devices, shards(): lax.all_gather(expert_down, 'exp', axis=1, tiled=True)  63.2 us
    all_to_all x1, starting transfers between devices, shards(): lax.all_to_all(outgoing, 'ctx', split_axis=0, concat_axis=0, tiled=True)  16.9 us
    all_to_all x1, starting transfers between devices, shards(): lax.all_to_all(result, 'ctx', split_axis=0, concat_axis=0, tiled=True)  16.2 us
    ppermute x3, waiting for transfers between devices, shifted(): return lax.ppermute(block, axis, route)  14 us
  transfers between devices with their start and end apart: 8, of which 6 were waited for; matrix products, arithmetic and copies ran while one was open for 1% of the time, Pallas kernels for 0%

commit v1 on v0

v1 whole, which is shorter than its diff:
```python
import math
import jax
import jax.numpy as jnp
from jax import lax
from jax.experimental import pallas as pl
from jax.sharding import PartitionSpec as P

HEAD = 128
TOP = 6
CAP = 16
BOTH = ("ctx", "exp")
ZH, NX, NY, ZL, NC = 4, 4, 4, 4, 2
NZ = ZH * ZL
PLANE = NX * NY


def join(z, x, y, c):
    zh, zl = z // ZL, z % ZL
    return ((zh * NX + x) * NY + y) * (ZL * NC) + zl * NC + c


def route(target):
    return [
        (join(z, x, y, c), join(*target(z, x, y, c)))
        for z in range(NZ)
        for x in range(NX)
        for y in range(NY)
        for c in range(NC)
    ]


SWAP = route(lambda z, x, y, c: (z, x, y, 1 - c))
RING = route(lambda z, x, y, c: ((z + 1 - 2 * c) % NZ, x, y, c))


def send(block, pairs):
    return lax.ppermute(block, BOTH, pairs)


def shifted(block, axis, distance):
    devices = range(lax.axis_size(axis))
    pairs = [(i - distance, i) for i in devices if i - distance in devices]
    return lax.ppermute(block, axis, pairs)


def attend(query_rows, key_rows, value_rows, query_marks, key_marks):
    shard_len, width = query_rows.shape
    block_rows = min(256, shard_len)
    span = shard_len + block_rows
    scale = HEAD ** (-0.5) * math.log2(math.e)

    def kernel(q_ref, k_ref, v_ref, mq_ref, mk_ref, out_ref):
        window = pl.ds(pl.multiple_of(pl.program_id(1) * block_rows, block_rows), span)
        scores = lax.dot_general(
            q_ref[...],
            k_ref[window, :],
            (((1,), (1,)), ((), ())),
            preferred_element_type=jnp.float32,
        )
        row = lax.broadcasted_iota(jnp.int32, (block_rows, span), 0)
        column = lax.broadcasted_iota(jnp.int32, (block_rows, span), 1)
        allowed = (mk_ref[:, window] == mq_ref[...]) & (column - row <= shard_len)
        scores = jnp.where(allowed, scores, -1e30)
        row_max = jnp.max(scores, axis=1, keepdims=True)
        weights = jnp.exp2((scores - row_max) * scale)
        total = jnp.sum(weights, axis=1, keepdims=True)
        mixed = jnp.dot(
            weights.astype(jnp.bfloat16), v_ref[window, :], preferred_element_type=jnp.float32
        )
        out_ref[...] = (mixed / total).astype(out_ref.dtype)

    keys_here = key_rows.shape[0]
    return pl.pallas_call(
        kernel,
        grid=(width // HEAD, shard_len // block_rows),
        in_specs=[
            pl.BlockSpec((block_rows, HEAD), lambda h, b: (b, h)),
            pl.BlockSpec((keys_here, HEAD), lambda h, b: (0, h)),
            pl.BlockSpec((keys_here, HEAD), lambda h, b: (0, h)),
            pl.BlockSpec((block_rows, 1), lambda h, b: (b, 0)),
            pl.BlockSpec((1, keys_here), lambda h, b: (0, 0)),
        ],
        out_specs=pl.BlockSpec((block_rows, HEAD), lambda h, b: (b, h)),
        out_shape=jax.ShapeDtypeStruct(query_rows.shape, query_rows.dtype),
        cost_estimate=pl.CostEstimate(
            flops=4 * shard_len * span * width,
            bytes_accessed=8 * shard_len * width,
            transcendentals=shard_len * span * width // HEAD,
        ),
        name="attend",
    )(query_rows, key_rows, value_rows, query_marks[:, None], key_marks[None, :])


def coords():
    ctx, exp = lax.axis_index("ctx"), lax.axis_index("exp")
    zh, x, y = ctx // PLANE, (ctx // NY) % NX, ctx % NY
    zl, c = exp // NC, exp % NC
    return zh * ZL + zl, x, y, c, zl


def column_weights(expert_up, expert_down, z, c):
    own = jnp.concatenate([expert_up, expert_down], axis=0)
    other = send(own, SWAP)
    ordered = jnp.where(
        c == 0, jnp.concatenate([own, other], axis=1), jnp.concatenate([other, own], axis=1)
    )
    up = jnp.zeros((NZ,) + ordered.shape[1:], ordered.dtype)
    down = jnp.zeros_like(up)

    def put(up, down, block, where):
        where = jnp.remainder(where, NZ)
        return (
            lax.dynamic_update_slice(up, block[0:1], (where, 0, 0)),
            lax.dynamic_update_slice(down, block[1:2], (where, 0, 0)),
        )

    up, down = put(up, down, ordered, z)
    sign = 1 - 2 * c
    moving = ordered
    for step in range(1, NZ // 2):
        moving = send(moving, RING)
        crossed = send(moving, SWAP)
        up, down = put(up, down, moving, z - sign * step)
        up, down = put(up, down, crossed, z + sign * step)
    half = send(lax.dynamic_slice_in_dim(moving, c, 1, 0), RING)
    crossed = send(half, SWAP)
    last = jnp.where(
        c == 0, jnp.concatenate([half, crossed], 0), jnp.concatenate([crossed, half], 0)
    )
    up, down = put(up, down, last, z + NZ // 2)
    features = up.shape[-1]
    return up.reshape(ZH, -1, features), down.reshape(ZH, -1, features)


def rotated(blocks, shift):
    n = len(blocks)
    stacked = jnp.stack(blocks + blocks)
    return lax.dynamic_slice_in_dim(stacked, jnp.remainder(-shift, n), n, 0)


def whole_projection(out_proj, x, y, c, zl):
    rows = out_proj.shape[0] // PLANE
    width = out_proj.shape[1]
    piece = lax.dynamic_slice_in_dim(out_proj, (x * NY + y) * rows, rows, 0)

    def along_z(d):
        return route(lambda z, x, y, c: (z // ZL * ZL + (z % ZL - d) % ZL, x, y, c))

    def along_y(d):
        return route(lambda z, x, y, c: (z, x, (y - d) % NY, c))

    def along_x(d):
        return route(lambda z, x, y, c: (z, (x - d) % NX, y, c))

    line = rotated([piece] + [send(piece, along_z(d)) for d in (1, 2, 3)], zl)
    line = rotated([line] + [send(line, along_y(d)) for d in (1, 2, 3)], y)
    right, left = send(line, along_x(1)), send(line, along_x(3))
    opposite = jnp.concatenate(
        [send(right[:2], along_x(1)), send(left[2:], along_x(3))], axis=0
    )
    plane = rotated([line, right, opposite, left], x)
    crossed = send(plane, SWAP)
    both = jnp.where(
        c == 0, jnp.stack([plane, crossed]), jnp.stack([crossed, plane])
    )
    return jnp.transpose(both, (3, 0, 1, 2, 4, 5)).reshape(ZL * NC, PLANE * rows, width)


def shards(
    queries,
    keys,
    values,
    segment_ids,
    out_proj,
    residual,
    norm_gain,
    expert_ids,
    gate_weights,
    expert_up,
    expert_down,
):
    z, x, y, c, zl = coords()
    shard_len = queries.shape[0]
    heads_here = queries.shape[1] // HEAD
    seg_marks = segment_ids + 1
    early_keys, early_values, early_marks = shifted((keys, values, seg_marks), "ctx", 1)
    out_whole = whole_projection(out_proj, x, y, c, zl)
    up_whole, down_whole = column_weights(expert_up, expert_down, z, c)
    attention = attend(
        queries,
        jnp.concatenate([early_keys, keys]),
        jnp.concatenate([early_values, values]),
        seg_marks,
        jnp.concatenate([early_marks, seg_marks]),
    )
    groups = lax.axis_size("exp")
    tok_rows = shard_len // groups
    mine = lax.all_to_all(
        attention.reshape(groups, tok_rows, heads_here * HEAD), "exp", 0, 0, tiled=True
    )
    projected = jnp.einsum("etk,ekd->td", mine, out_whole, preferred_element_type=jnp.float32)
    stream = (residual.astype(jnp.float32) + projected).astype(jnp.bfloat16)
    stream_f = stream.astype(jnp.float32)
    mean_square = jnp.mean(stream_f * stream_f, axis=1, keepdims=True)
    normed = (stream_f * lax.rsqrt(mean_square + 1e-06) * norm_gain[None, :]).astype(jnp.bfloat16)
    feature_count = stream.shape[1]
    experts = lax.axis_size("ctx")
    slots = experts * CAP
    flat_ids = expert_ids.reshape(-1)
    one_hot = (flat_ids[:, None] == jnp.arange(experts, dtype=jnp.int32)[None, :]).astype(jnp.int32)
    earlier = jnp.cumsum(one_hot, axis=0) - one_hot
    slot_rank = jnp.sum(earlier * one_hot, axis=1)
    place = flat_ids % PLANE * ZH + flat_ids // PLANE
    slot_grid = (place * CAP + slot_rank).reshape(tok_rows, TOP)
    hits = slot_grid[:, :, None] == jnp.arange(slots, dtype=jnp.int32)[None, None, :]
    placing = jnp.any(hits, axis=1).astype(jnp.bfloat16)
    gates = jnp.sum(jnp.where(hits, gate_weights[:, :, None], 0.0), axis=1)
    gates_high = gates.astype(jnp.bfloat16)
    gates_low = (gates - gates_high.astype(jnp.float32)).astype(jnp.bfloat16)
    outgoing = lax.dot_general(
        placing, normed, (((0,), (0,)), ((), ())), preferred_element_type=jnp.float32
    ).astype(jnp.bfloat16)
    plane_groups = [[h * PLANE + p for p in range(PLANE)] for h in range(ZH)]
    arrived = lax.all_to_all(
        outgoing.reshape(PLANE, ZH * CAP, feature_count),
        "ctx",
        0,
        0,
        axis_index_groups=plane_groups,
        tiled=True,
    )
    rows = arrived.reshape(PLANE, ZH, CAP, feature_count).transpose(1, 0, 2, 3)
    rows = rows.reshape(ZH, PLANE * CAP, feature_count)
    hidden = jax.nn.silu(
        jnp.einsum("hrd,hfd->hrf", rows, up_whole, preferred_element_type=jnp.float32)
    ).astype(jnp.bfloat16)
    result = jnp.einsum(
        "hrf,hfd->hrd", hidden, down_whole, preferred_element_type=jnp.float32
    ).astype(jnp.bfloat16)
    result = result.reshape(ZH, PLANE, CAP, feature_count).transpose(1, 0, 2, 3)
    returned = lax.all_to_all(
        result.reshape(PLANE, ZH * CAP, feature_count),
        "ctx",
        0,
        0,
        axis_index_groups=plane_groups,
        tiled=True,
    ).reshape(slots, feature_count)
    mixture = jnp.dot(gates_high, returned, preferred_element_type=jnp.float32) + jnp.dot(
        gates_low, returned, preferred_element_type=jnp.float32
    )
    return (stream_f + mixture).astype(jnp.bfloat16)


def solution(mesh):
    in_specs = (
        P("ctx", "exp"),
        P("ctx", "exp"),
        P("ctx", "exp"),
        P("ctx"),
        P("exp", None),
        P(("ctx", "exp"), None),
        P(),
        P(("ctx", "exp"), None),
        P(("ctx", "exp"), None),
        P("ctx", "exp", None),
        P("ctx", "exp", None),
    )
    out_specs = P(("ctx", "exp"), None)
    return jax.shard_map(shards, mesh=mesh, in_specs=in_specs, out_specs=out_specs, check_vma=False)
```

time: 557 us -> 374 us (0.67)
  waiting for transfers between devices: 431 us -> 101 us
  starting transfers between devices: 43.5 us -> 165 us
  local copies, waits for them, and re-layouts: 18.8 us -> 57 us
  between operations: 13.4 us -> 0.63 us
  Pallas kernels: 0 us -> 9.76 us
  matrix products: 28.7 us -> 21.1 us
    all_gather x2 -> x0, waiting for transfers between devices: 173 us -> none  [the longest x1 110 us: shards(): lax.all_gather(expert_up, 'exp', axis=1, tiled=True)]
    ppermute x3 -> x31, starting transfers between devices: 10.2 us -> 147 us  [the longest x28 139 us: send(): return lax.ppermute(block, BOTH, pairs)]
    reduce_scatter x1 -> x0, waiting for transfers between devices: 120 us -> none  [shards(): lax.psum_scatter(jnp.dot(row_block, out_proj, preferred_element_type=jnp....]
    all_to_all x2 -> x3, waiting for transfers between devices: 122 us -> 33.5 us  [the longest x1 33.4 us: shards(): lax.all_to_all(result.reshape(PLANE, ZH * CAP, feature_count), 'ctx', 0,...]
    ppermute x3 -> x31, waiting for transfers between devices: 14 us -> 67.4 us  [the longest x28 67.4 us: send(): return lax.ppermute(block, BOTH, pairs)]
    dynamic_update_slice x0 -> x17, local copies, waits for them, and re-layouts: none -> 24.5 us  [the longest x16 23.6 us: put(): lax.dynamic_update_slice(up, block[0:1], (where, 0, 0))]
    all_to_all x2 -> x3, starting transfers between devices: 33 us -> 17.4 us  [the longest x1 7.05 us: shards(): lax.all_to_all(attention.reshape(groups, tok_rows, heads_here * HEAD), 'e...]
    unnamed x18 -> x37, local copies, waits for them, and re-layouts: 0.26 us -> 13 us
  transfers between devices with their start and end apart: 8 -> 34, of which waited for: 6 -> 10; matrix products, arithmetic and copies ran while one was open for 1% -> 20% of each run, Pallas kernels for 0% -> 3%
where the time goes in v1:
time: 374 us; the launch traced here: 372 us
  starting transfers between devices  165 us (44%)
  waiting for transfers between devices  101 us (27%)
  local copies, waits for them, and re-layouts  57 us (15%)
  matrix products  21.1 us (6%)
  other arithmetic  18 us (5%)
  Pallas kernels  9.76 us (3%)
    ppermute x28, starting transfers between devices, send(): return lax.ppermute(block, BOTH, pairs)  139 us
    ppermute x28, waiting for transfers between devices, send(): return lax.ppermute(block, BOTH, pairs)  67.4 us
    all_to_all x1, waiting for transfers between devices, shards(): lax.all_to_all(result.reshape(PLANE, ZH * CAP, feature_count), 'ctx', 0,...  33.4 us
    dynamic_update_slice x16, local copies, waits for them, and re-layouts, put(): lax.dynamic_update_slice(up, block[0:1], (where, 0, 0))  23.6 us
    unnamed x37, local copies, waits for them, and re-layouts  13 us
    dot_general x1, matrix products, shards(): jnp.einsum('hrf,hfd->hrd', hidden, down_whole, preferred_element_type=jnp...  11.2 us
    pallas_call x1, Pallas kernels, attend(): pl.pallas_call(kernel, grid=(width // HEAD, shard_len // block_rows), in_...  9.76 us
    ppermute x3, starting transfers between devices, shifted(): return lax.ppermute(block, axis, pairs)  8.11 us
  transfers between devices with their start and end apart: 34, of which 10 were waited for; matrix products, arithmetic and copies ran while one was open for 20% of the time, Pallas kernels for 3%

profile of v1, /device:TPU:1, one launch (start us, length us, event | category | flops | bytes accessed | tf_op | source)
XLA Modules:
  0.0 371.9 jit_solution(2249848301392362423)
XLA Ops:
  0.8 7.1 %collective-permute-start.3 = (bf16[16,1280]{1,0:T(8,128)(2,1)S(1)}, bf16[16,1280]{1,0:T(8,128)(2,1)S(1)}, u32[]{:S(2)}, u32[]{:S(2)}) collective-permute-start(bf16[16,1280]{1,0:T(8,128)(2,1)S(1)} %get-tuple-element.10), channel_id=1, source_target_pairs={{0,6},{1,7},{8,14},{9,15},{16,22},{17,23},{24,30},{25,31},{32,38},... | collective-permute-start | bytes 122888 | tf_op jit(solution)/shard_map/ppermute | solution.py:37
  13.9 5.3 %collective-permute-start.14 = (bf16[2,96,1280]{2,1,0:T(8,128)(2,1)S(1)}, bf16[2,96,1280]{2,1,0:T(8,128)(2,1)}, u32[]{:S(2)}, u32[]{:S(2)}) collective-permute-start(bf16[2,96,1280]{2,1,0:T(8,128)(2,1)S(1)} %constant_dynamic-update-slice_fusion.8), channel_id=1, source_target_pairs={{0,1},{1,0},{8,9},{9,8},{16,17},{17,16},{24,25},{25,24},{32,33},{3... | collective-permute-start | bytes 1474568 | tf_op jit(solution)/shard_map/ppermute | solution.py:37
  24.9 3.8 %collective-permute-start = (bf16[1024,256]{1,0:T(8,128)(2,1)}, bf16[1024,256]{1,0:T(8,128)(2,1)}, u32[]{:S(2)}, u32[]{:S(2)}) collective-permute-start(bf16[1024,256]{1,0:T(8,128)(2,1)} %param.12), channel_id=1, source_target_pairs={{0,8},{8,16},{16,24},{24,32},{32,40},{40,48},{48,56},{56,64},{64,7... | collective-permute-start | bytes 1572872 | tf_op jit(solution)/shard_map/ppermute | solution.py:43
  28.7 3.0 collective-permute-start.1
  32.5 3.7 collective-permute-start.6
  40.9 2.6 collective-permute-start.8
  44.2 12.6 %collective-permute-done.7 = bf16[4,16,1280]{2,1,0:T(8,128)(2,1)S(1)} collective-permute-done((bf16[4,16,1280]{2,1,0:T(8,128)(2,1)S(1)}, bf16[4,16,1280]{2,1,0:T(8,128)(2,1)S(1)}, u32[]{:S(2)}, u32[]{:S(2)}) %collective-permute-start.7) | collective-permute-done | bytes 163872 | tf_op jit(solution)/shard_map/ppermute | solution.py:37
  62.9 10.0 %collective-permute-start.9 = (bf16[4,4,16,1280]{3,2,0,1:T(8,128)(2,1)S(1)}, bf16[4,4,16,1280]{3,2,0,1:T(8,128)(2,1)S(1)}, u32[]{:S(2)}, u32[]{:S(2)}) collective-permute-start(bf16[4,4,16,1280]{3,2,0,1:T(8,128)(2,1)S(1)} %get-tuple-element.6), channel_id=1, source_target_pairs={{0,96},{1,97},{8,104},{9,105},{16,112},{17,113},{24,120},{25,121},... | collective-permute-start | bytes 1966088 | tf_op jit(solution)/shard_map/ppermute | solution.py:37
  76.4 8.1 %collective-permute-start.15 = (bf16[2,192,1280]{2,1,0:T(8,128)(2,1)S(1)}, bf16[2,192,1280]{2,1,0:T(8,128)(2,1)}, u32[]{:S(2)}, u32[]{:S(2)}) collective-permute-start(bf16[2,192,1280]{2,1,0:T(8,128)(2,1)S(1)} %maximum_select_fusion.1), channel_id=1, source_target_pairs={{0,2},{1,391},{8,10},{9,399},{16,18},{17,407},{24,26},{25,415},{32... | collective-permute-start | bytes 2949128 | tf_op jit(solution)/shard_map/ppermute | solution.py:37
  84.6 3.8 %broadcast.101.clone.1 = bf16[16,192,1280]{2,1,0:T(8,128)(2,1)} broadcast(bf16[]{:T(256)} %constant.191.clone.1), dimensions={} | broadcast | bytes 7864322 | tf_op jit(solution)/shard_map/broadcast.5
  89.2 3.8 %broadcast.101.clone = bf16[16,192,1280]{2,1,0:T(8,128)(2,1)} broadcast(bf16[]{:T(256)} %constant.191.clone.1), dimensions={} | broadcast | bytes 7864322 | tf_op jit(solution)/shard_map/broadcast.5
  98.1 9.8 %attend.1 = bf16[1024,256]{1,0:T(8,128)(2,1)} custom-call(bf16[1024,256]{1,0:T(8,128)(2,1)} %q_ref.1, bf16[2048,256]{1,0:T(8,128)(2,1)} %pad_maximum_fusion.k_ref, bf16[2048,256]{1,0:T(8,128)(2,1)} %pad_maximum_fusion.1.v_ref, s32[1024,1]{1,0:T(8,128)} %copy.34.mq_ref, s32[1,2048]{1,0:T(1,128)} %bitcast.120), custom_call_target="tpu_custom_call" | custom-call | flops 1342177280 | bytes 2097152 | tf_op jit(solution)/shard_map/attend/pallas_call | solution.py:73
  107.9 7.0 %all-to-all-start = ((bf16[8,128,256]{2,1,0:T(8,128)(2,1)}), bf16[8,128,256]{2,1,0:T(8,128)(2,1)S(1)}, u32[]{:S(2)}, u32[]{:S(2)}) async-start(bf16[8,128,256]{2,1,0:T(8,128)(2,1)} %bitcast.117), calls=%async_computation | async-start | bytes 1048576 | tf_op jit(solution)/shard_map/all_to_all | solution.py:198
  114.9 2.9 collective-permute-start.10
  117.8 2.4 collective-permute-start.12
  121.2 4.9 %collective-permute-done.10 = bf16[2,4,16,1280]{3,2,0,1:T(8,128)(2,1)S(1)} collective-permute-done((bf16[2,4,16,1280]{3,2,0,1:T(8,128)(2,1)S(1)}, bf16[2,4,16,1280]{3,2,0,1:T(8,128)(2,1)S(1)}, u32[]{:S(2)}, u32[]{:S(2)}) %collective-permute-start.10) | collective-permute-done | bytes 327712 | tf_op jit(solution)/shard_map/ppermute | solution.py:37
  126.1 3.8 %collective-permute-done.12 = bf16[2,4,16,1280]{3,2,0,1:T(8,128)(2,1)S(1)} collective-permute-done((bf16[2,4,16,1280]{3,2,0,1:T(8,128)(2,1)S(1)}, bf16[2,4,16,1280]{3,2,0,1:T(8,128)(2,1)S(1)}, u32[]{:S(2)}, u32[]{:S(2)}) %collective-permute-start.12) | collective-permute-done | bytes 327712 | tf_op jit(solution)/shard_map/ppermute | solution.py:37
  135.3 3.3 collective-permute-start.16
  138.6 39.0 %collective-permute-start.17 = (bf16[2,192,1280]{2,1,0:T(8,128)(2,1)}, bf16[2,192,1280]{2,1,0:T(8,128)(2,1)S(1)}, u32[]{:S(2)}, u32[]{:S(2)}) collective-permute-start(bf16[2,192,1280]{2,1,0:T(8,128)(2,1)} %collective-permute-done.15), channel_id=1, source_target_pairs={{0,2},{1,391},{8,10},{9,399},{16,18},{17,407},{24,26},{25,415},{32... | collective-permute-start | bytes 2949128 | tf_op jit(solution)/shard_map/ppermute | solution.py:37
  181.7 2.3 slice_dynamic-update-slice_fusion.30
  183.9 5.0 %collective-permute-done.17 = bf16[2,192,1280]{2,1,0:T(8,128)(2,1)S(1)} collective-permute-done((bf16[2,192,1280]{2,1,0:T(8,128)(2,1)}, bf16[2,192,1280]{2,1,0:T(8,128)(2,1)S(1)}, u32[]{:S(2)}, u32[]{:S(2)}) %collective-permute-start.17) | collective-permute-done | bytes 983072 | tf_op jit(solution)/shard_map/ppermute | solution.py:37
  188.9 3.3 collective-permute-start.18
  192.2 3.6 collective-permute-start.19
  197.9 9.5 %collective-permute-done.19 = bf16[2,192,1280]{2,1,0:T(8,128)(2,1)} collective-permute-done((bf16[2,192,1280]{2,1,0:T(8,128)(2,1)S(1)}, bf16[2,192,1280]{2,1,0:T(8,128)(2,1)}, u32[]{:S(2)}, u32[]{:S(2)}) %collective-permute-start.19) | collective-permute-done | bytes 983072 | tf_op jit(solution)/shard_map/ppermute | solution.py:37
  207.4 4.0 %collective-permute-start.20 = (bf16[2,192,1280]{2,1,0:T(8,128)(2,1)}, bf16[2,192,1280]{2,1,0:T(8,128)(2,1)}, u32[]{:S(2)}, u32[]{:S(2)}) collective-permute-start(bf16[2,192,1280]{2,1,0:T(8,128)(2,1)} %collective-permute-done.19), channel_id=1, source_target_pairs={{0,1},{1,0},{8,9},{9,8},{16,17},{17,16},{24,25},{25,24},{32,33},{3... | collective-permute-start | bytes 2949128 | tf_op jit(solution)/shard_map/ppermute | solution.py:37
  211.4 2.8 collective-permute-start.21
  217.5 3.0 maximum_select_fusion
  220.5 3.5 multiply_reduce_fusion
  224.0 2.4 convolution_convert_fusion.1
  226.5 3.7 %all-to-all-start.1 = ((bf16[16,64,1280]{2,1,0:T(8,128)(2,1)}), bf16[16,64,1280]{2,1,0:T(8,128)(2,1)S(1)}, u32[]{:S(2)}, u32[]{:S(2)}) async-start(bf16[16,64,1280]{2,1,0:T(8,128)(2,1)} %bitcast.112), calls=%async_computation.1 | async-start | bytes 5242880 | tf_op jit(solution)/shard_map/all_to_all | solution.py:224
  232.1 3.9 %collective-permute-start.23 = (bf16[2,192,1280]{2,1,0:T(8,128)(2,1)}, bf16[2,192,1280]{2,1,0:T(8,128)(2,1)S(1)}, u32[]{:S(2)}, u32[]{:S(2)}) collective-permute-start(bf16[2,192,1280]{2,1,0:T(8,128)(2,1)} %collective-permute-done.21), channel_id=1, source_target_pairs={{0,2},{1,391},{8,10},{9,399},{16,18},{17,407},{24,26},{25,415},{32... | collective-permute-start | bytes 2949128 | tf_op jit(solution)/shard_map/ppermute | solution.py:37
  240.5 7.0 %collective-permute-done.23 = bf16[2,192,1280]{2,1,0:T(8,128)(2,1)S(1)} collective-permute-done((bf16[2,192,1280]{2,1,0:T(8,128)(2,1)}, bf16[2,192,1280]{2,1,0:T(8,128)(2,1)S(1)}, u32[]{:S(2)}, u32[]{:S(2)}) %collective-permute-start.23) | collective-permute-done | bytes 983072 | tf_op jit(solution)/shard_map/ppermute | solution.py:37
  247.5 4.5 %collective-permute-start.24 = (bf16[2,192,1280]{2,1,0:T(8,128)(2,1)S(1)}, bf16[2,192,1280]{2,1,0:T(8,128)(2,1)S(1)}, u32[]{:S(2)}, u32[]{:S(2)}) collective-permute-start(bf16[2,192,1280]{2,1,0:T(8,128)(2,1)S(1)} %collective-permute-done.23), channel_id=1, source_target_pairs={{0,1},{1,0},{8,9},{9,8},{16,17},{17,16},{24,25},{25,24},{32,33},{3... | collective-permute-start | bytes 2949128 | tf_op jit(solution)/shard_map/ppermute | solution.py:37
  251.9 2.6 collective-permute-start.25
  256.6 10.5 %collective-permute-done.25 = bf16[2,192,1280]{2,1,0:T(8,128)(2,1)S(1)} collective-permute-done((bf16[2,192,1280]{2,1,0:T(8,128)(2,1)S(1)}, bf16[2,192,1280]{2,1,0:T(8,128)(2,1)S(1)}, u32[]{:S(2)}, u32[]{:S(2)}) %collective-permute-start.25) | collective-permute-done | bytes 983072 | tf_op jit(solution)/shard_map/ppermute | solution.py:37
  267.1 4.2 %collective-permute-start.26 = (bf16[2,192,1280]{2,1,0:T(8,128)(2,1)S(1)}, bf16[2,192,1280]{2,1,0:T(8,128)(2,1)S(1)}, u32[]{:S(2)}, u32[]{:S(2)}) collective-permute-start(bf16[2,192,1280]{2,1,0:T(8,128)(2,1)S(1)} %collective-permute-done.25), channel_id=1, source_target_pairs={{0,1},{1,0},{8,9},{9,8},{16,17},{17,16},{24,25},{25,24},{32,33},{3... | collective-permute-start | bytes 2949128 | tf_op jit(solution)/shard_map/ppermute | solution.py:37
  276.3 10.2 %collective-permute-done.27 = bf16[2,192,1280]{2,1,0:T(8,128)(2,1)} collective-permute-done((bf16[2,192,1280]{2,1,0:T(8,128)(2,1)S(1)}, bf16[2,192,1280]{2,1,0:T(8,128)(2,1)}, u32[]{:S(2)}, u32[]{:S(2)}) %collective-permute-start.27) | collective-permute-done | bytes 983072 | tf_op jit(solution)/shard_map/ppermute | solution.py:37
  286.5 2.4 slice_dynamic-update-slice_fusion.18
  288.9 2.9 collective-permute-start.29
  291.7 3.1 collective-permute-start.28
  294.8 4.0 %collective-permute-done.29 = bf16[1,192,1280]{2,1,0:T(8,128)(2,1)} collective-permute-done((bf16[1,192,1280]{2,1,0:T(8,128)(2,1)S(1)}, bf16[1,192,1280]{2,1,0:T(8,128)(2,1)}, u32[]{:S(2)}, u32[]{:S(2)}) %collective-permute-start.29) | collective-permute-done | bytes 491552 | tf_op jit(solution)/shard_map/ppermute | solution.py:37
  298.8 6.1 %collective-permute-start.30 = (bf16[1,192,1280]{2,1,0:T(8,128)(2,1)}, bf16[1,192,1280]{2,1,0:T(8,128)(2,1)}, u32[]{:S(2)}, u32[]{:S(2)}) collective-permute-start(bf16[1,192,1280]{2,1,0:T(8,128)(2,1)} %collective-permute-done.29), channel_id=1, source_target_pairs={{0,1},{1,0},{8,9},{9,8},{16,17},{17,16},{24,25},{25,24},{32,33},{3... | collective-permute-start | bytes 1474568 | tf_op jit(solution)/shard_map/ppermute | solution.py:37
  308.6 2.3 slice_dynamic-update-slice_fusion.17
  311.9 11.2 %convolution_convert_fusion = bf16[4,256,1280]{2,1,0:T(8,128)(2,1)} fusion(bf16[4,768,1280]{2,1,0:T(8,128)(2,1)} %bitcast.34, bf16[4,256,1280]{2,1,0:T(8,128)(2,1)S(1)} %bitcast.114, bf16[4,768,1280]{2,1,0:T(8,128)(2,1)} %bitcast.33), kind=kOutput, calls=%fused_computation.1 | convolution fusion | flops 4031774720 | bytes 20971520 | tf_op jit(solution)/shard_map/hrf,hfd->hrd/dot_general | solution.py:237
  323.1 3.5 copy.52
  326.6 6.6 %all-to-all-start.2 = ((bf16[16,64,1280]{2,1,0:T(8,128)(2,1)}), bf16[16,64,1280]{2,1,0:T(8,128)(2,1)S(1)}, u32[]{:S(2)}, u32[]{:S(2)}) async-start(bf16[16,64,1280]{2,1,0:T(8,128)(2,1)} %bitcast.113), calls=%async_computation.2 | async-start | bytes 5242880 | tf_op jit(solution)/shard_map/all_to_all | solution.py:241
  334.5 33.4 %all-to-all-done.2 = bf16[16,64,1280]{2,1,0:T(8,128)(2,1)S(1)} async-done(((bf16[16,64,1280]{2,1,0:T(8,128)(2,1)}), bf16[16,64,1280]{2,1,0:T(8,128)(2,1)S(1)}, u32[]{:S(2)}, u32[]{:S(2)}) %all-to-all-start.2) | async-done | bytes 2621472 | tf_op jit(solution)/shard_map/all_to_all | solution.py:241
  369.5 2.5 fusion.3
  (115 shorter events, 70.6 us)
Async XLA Ops:
  0.8 24.1 %collective-permute-start.3 = (bf16[16,1280]{1,0:T(8,128)(2,1)S(1)}, bf16[16,1280]{1,0:T(8,128)(2,1)S(1)}, u32[]{:S(2)}, u32[]{:S(2)}) collective-permute-start(bf16[16,1280]{1,0:T(8,128)(2,1)S(1)} %get-tuple-element.10), channel_id=1, source_target_pairs={{0,6},{1,7},{8,14},{9,15},{16,22},{17,23},{24,30},{25,31},{32,38},... | collective-permute-start | bytes 122888 | tf_op jit(solution)/shard_map/ppermute | solution.py:37
  7.9 20.9 %collective-permute-start.4 = (bf16[16,1280]{1,0:T(8,128)(2,1)S(1)}, bf16[16,1280]{1,0:T(8,128)(2,1)S(1)}, u32[]{:S(2)}, u32[]{:S(2)}) collective-permute-start(bf16[16,1280]{1,0:T(8,128)(2,1)S(1)} %get-tuple-element.10), channel_id=1, source_target_pairs={{0,4},{1,5},{8,12},{9,13},{16,20},{17,21},{24,28},{25,29},{32,36},... | collective-permute-start | bytes 122888 | tf_op jit(solution)/shard_map/ppermute | solution.py:37
  9.8 21.9 %collective-permute-start.5 = (bf16[16,1280]{1,0:T(8,128)(2,1)S(1)}, bf16[16,1280]{1,0:T(8,128)(2,1)S(1)}, u32[]{:S(2)}, u32[]{:S(2)}) collective-permute-start(bf16[16,1280]{1,0:T(8,128)(2,1)S(1)} %get-tuple-element.10), channel_id=1, source_target_pairs={{0,2},{1,3},{8,10},{9,11},{16,18},{17,19},{24,26},{25,27},{32,34},... | collective-permute-start | bytes 122888 | tf_op jit(solution)/shard_map/ppermute | solution.py:37
  13.9 61.0 %collective-permute-start.14 = (bf16[2,96,1280]{2,1,0:T(8,128)(2,1)S(1)}, bf16[2,96,1280]{2,1,0:T(8,128)(2,1)}, u32[]{:S(2)}, u32[]{:S(2)}) collective-permute-start(bf16[2,96,1280]{2,1,0:T(8,128)(2,1)S(1)} %constant_dynamic-update-slice_fusion.8), channel_id=1, source_target_pairs={{0,1},{1,0},{8,9},{9,8},{16,17},{17,16},{24,25},{25,24},{32,33},{3... | collective-permute-start | bytes 1474568 | tf_op jit(solution)/shard_map/ppermute | solution.py:37
  19.9 18.4 %collective-permute-start.2 = (s32[1024]{0:T(1024)S(1)}, s32[1024]{0:T(1024)S(1)}, u32[]{:S(2)}, u32[]{:S(2)}) collective-permute-start(s32[1024]{0:T(1024)S(1)} %broadcast_add_fusion), channel_id=1, source_target_pairs={{0,8},{8,16},{16,24},{24,32},{32,40},{40,48},{48,56},{56,64},{64,7... | collective-permute-start | bytes 12296 | tf_op jit(solution)/shard_map/ppermute | solution.py:43
  24.9 69.0 %collective-permute-start = (bf16[1024,256]{1,0:T(8,128)(2,1)}, bf16[1024,256]{1,0:T(8,128)(2,1)}, u32[]{:S(2)}, u32[]{:S(2)}) collective-permute-start(bf16[1024,256]{1,0:T(8,128)(2,1)} %param.12), channel_id=1, source_target_pairs={{0,8},{8,16},{16,24},{24,32},{32,40},{40,48},{48,56},{56,64},{64,7... | collective-permute-start | bytes 1572872 | tf_op jit(solution)/shard_map/ppermute | solution.py:43
  28.7 67.3 %collective-permute-start.1 = (bf16[1024,256]{1,0:T(8,128)(2,1)}, bf16[1024,256]{1,0:T(8,128)(2,1)}, u32[]{:S(2)}, u32[]{:S(2)}) collective-permute-start(bf16[1024,256]{1,0:T(8,128)(2,1)} %param.13), channel_id=1, source_target_pairs={{0,8},{8,16},{16,24},{24,32},{32,40},{40,48},{48,56},{56,64},{64,7... | collective-permute-start | bytes 1572872 | tf_op jit(solution)/shard_map/ppermute | solution.py:43
  32.5 8.5 %collective-permute-start.6 = (bf16[4,16,1280]{2,1,0:T(8,128)(2,1)S(1)}, bf16[4,16,1280]{2,1,0:T(8,128)(2,1)S(1)}, u32[]{:S(2)}, u32[]{:S(2)}) collective-permute-start(bf16[4,16,1280]{2,1,0:T(8,128)(2,1)S(1)} %get-tuple-element.8), channel_id=1, source_target_pairs={{0,24},{1,25},{8,0},{9,1},{16,8},{17,9},{24,16},{25,17},{32,56},{3... | collective-permute-start | bytes 491528 | tf_op jit(solution)/shard_map/ppermute | solution.py:37
  39.0 17.8 %collective-permute-start.7 = (bf16[4,16,1280]{2,1,0:T(8,128)(2,1)S(1)}, bf16[4,16,1280]{2,1,0:T(8,128)(2,1)S(1)}, u32[]{:S(2)}, u32[]{:S(2)}) collective-permute-start(bf16[4,16,1280]{2,1,0:T(8,128)(2,1)S(1)} %get-tuple-element.8), channel_id=1, source_target_pairs={{0,16},{1,17},{8,24},{9,25},{16,0},{17,1},{24,8},{25,9},{32,48},{3... | collective-permute-start | bytes 491528 | tf_op jit(solution)/shard_map/ppermute | solution.py:37
  40.9 16.5 %collective-permute-start.8 = (bf16[4,16,1280]{2,1,0:T(8,128)(2,1)S(1)}, bf16[4,16,1280]{2,1,0:T(8,128)(2,1)S(1)}, u32[]{:S(2)}, u32[]{:S(2)}) collective-permute-start(bf16[4,16,1280]{2,1,0:T(8,128)(2,1)S(1)} %get-tuple-element.8), channel_id=1, source_target_pairs={{0,8},{1,9},{8,16},{9,17},{16,24},{17,25},{24,0},{25,1},{32,40},{3... | collective-permute-start | bytes 491528 | tf_op jit(solution)/shard_map/ppermute | solution.py:37
  62.9 52.0 %collective-permute-start.9 = (bf16[4,4,16,1280]{3,2,0,1:T(8,128)(2,1)S(1)}, bf16[4,4,16,1280]{3,2,0,1:T(8,128)(2,1)S(1)}, u32[]{:S(2)}, u32[]{:S(2)}) collective-permute-start(bf16[4,4,16,1280]{3,2,0,1:T(8,128)(2,1)S(1)} %get-tuple-element.6), channel_id=1, source_target_pairs={{0,96},{1,97},{8,104},{9,105},{16,112},{17,113},{24,120},{25,121},... | collective-permute-start | bytes 1966088 | tf_op jit(solution)/shard_map/ppermute | solution.py:37
  72.9 44.9 %collective-permute-start.11 = (bf16[4,4,16,1280]{3,2,0,1:T(8,128)(2,1)S(1)}, bf16[4,4,16,1280]{3,2,0,1:T(8,128)(2,1)S(1)}, u32[]{:S(2)}, u32[]{:S(2)}) collective-permute-start(bf16[4,4,16,1280]{3,2,0,1:T(8,128)(2,1)S(1)} %get-tuple-element.6), channel_id=1, source_target_pairs={{0,32},{1,33},{8,40},{9,41},{16,48},{17,49},{24,56},{25,57},{32,64... | collective-permute-start | bytes 1966088 | tf_op jit(solution)/shard_map/ppermute | solution.py:37
  76.4 58.9 %collective-permute-start.15 = (bf16[2,192,1280]{2,1,0:T(8,128)(2,1)S(1)}, bf16[2,192,1280]{2,1,0:T(8,128)(2,1)}, u32[]{:S(2)}, u32[]{:S(2)}) collective-permute-start(bf16[2,192,1280]{2,1,0:T(8,128)(2,1)S(1)} %maximum_select_fusion.1), channel_id=1, source_target_pairs={{0,2},{1,391},{8,10},{9,399},{16,18},{17,407},{24,26},{25,415},{32... | collective-permute-start | bytes 2949128 | tf_op jit(solution)/shard_map/ppermute | solution.py:37
  88.4 5.5 %copy-start.3 = (bf16[1024,256]{1,0:T(8,128)(2,1)S(1)}, bf16[1024,256]{1,0:T(8,128)(2,1)}, u32[]{:S(2)}) copy-start(bf16[1024,256]{1,0:T(8,128)(2,1)} %param.12) | copy-start | bytes 1572868
  89.2 6.7 %copy-start.4 = (bf16[1024,256]{1,0:T(8,128)(2,1)S(1)}, bf16[1024,256]{1,0:T(8,128)(2,1)}, u32[]{:S(2)}) copy-start(bf16[1024,256]{1,0:T(8,128)(2,1)} %param.13) | copy-start | bytes 1572868
  107.9 112.7 %all-to-all-start = ((bf16[8,128,256]{2,1,0:T(8,128)(2,1)}), bf16[8,128,256]{2,1,0:T(8,128)(2,1)S(1)}, u32[]{:S(2)}, u32[]{:S(2)}) async-start(bf16[8,128,256]{2,1,0:T(8,128)(2,1)} %bitcast.117), calls=%async_computation | async-start | bytes 1048576 | tf_op jit(solution)/shard_map/all_to_all | solution.py:198
  114.9 11.1 %collective-permute-start.10 = (bf16[2,4,16,1280]{3,2,0,1:T(8,128)(2,1)S(1)}, bf16[2,4,16,1280]{3,2,0,1:T(8,128)(2,1)S(1)}, u32[]{:S(2)}, u32[]{:S(2)}) collective-permute-start(bf16[2,4,16,1280]{3,2,0,1:T(8,128)(2,1)S(1)} %slice.144), channel_id=1, source_target_pairs={{0,96},{1,97},{8,104},{9,105},{16,112},{17,113},{24,120},{25,121},... | collective-permute-start | bytes 983048 | tf_op jit(solution)/shard_map/ppermute | solution.py:37
  117.8 12.1 %collective-permute-start.12 = (bf16[2,4,16,1280]{3,2,0,1:T(8,128)(2,1)S(1)}, bf16[2,4,16,1280]{3,2,0,1:T(8,128)(2,1)S(1)}, u32[]{:S(2)}, u32[]{:S(2)}) collective-permute-start(bf16[2,4,16,1280]{3,2,0,1:T(8,128)(2,1)S(1)} %slice.145), channel_id=1, source_target_pairs={{0,32},{1,33},{8,40},{9,41},{16,48},{17,49},{24,56},{25,57},{32,64... | collective-permute-start | bytes 983048 | tf_op jit(solution)/shard_map/ppermute | solution.py:37
  135.3 46.2 %copy-start = (bf16[8,4,4,16,1280]{4,3,1,0,2:T(8,128)(2,1)S(1)}, bf16[8,4,4,16,1280]{4,3,1,0,2:T(8,128)(2,1)}, u32[]{:S(2)}) copy-start(bf16[8,4,4,16,1280]{4,3,1,0,2:T(8,128)(2,1)} %bitcast_dynamic-update-slice_fusion.3) | copy-start | bytes 15728644
  135.3 60.5 %collective-permute-start.16 = (bf16[2,192,1280]{2,1,0:T(8,128)(2,1)}, bf16[2,192,1280]{2,1,0:T(8,128)(2,1)S(1)}, u32[]{:S(2)}, u32[]{:S(2)}) collective-permute-start(bf16[2,192,1280]{2,1,0:T(8,128)(2,1)} %collective-permute-done.15), channel_id=1, source_target_pairs={{0,1},{1,0},{8,9},{9,8},{16,17},{17,16},{24,25},{25,24},{32,33},{3... | collective-permute-start | bytes 2949128 | tf_op jit(solution)/shard_map/ppermute | solution.py:37
  138.6 50.3 %collective-permute-start.17 = (bf16[2,192,1280]{2,1,0:T(8,128)(2,1)}, bf16[2,192,1280]{2,1,0:T(8,128)(2,1)S(1)}, u32[]{:S(2)}, u32[]{:S(2)}) collective-permute-start(bf16[2,192,1280]{2,1,0:T(8,128)(2,1)} %collective-permute-done.15), channel_id=1, source_target_pairs={{0,2},{1,391},{8,10},{9,399},{16,18},{17,407},{24,26},{25,415},{32... | collective-permute-start | bytes 2949128 | tf_op jit(solution)/shard_map/ppermute | solution.py:37
  179.5 38.0 %collective-permute-start.13 = (bf16[4,4,4,16,1280]{4,3,1,0,2:T(8,128)(2,1)S(1)}, bf16[4,4,4,16,1280]{4,3,1,0,2:T(8,128)(2,1)S(1)}, u32[]{:S(2)}, u32[]{:S(2)}) collective-permute-start(bf16[4,4,4,16,1280]{4,3,1,0,2:T(8,128)(2,1)S(1)} %constant_dynamic-slice_fusion.1), channel_id=1, source_target_pairs={{0,1},{1,0},{8,9},{9,8},{16,17},{17,16},{24,25},{25,24},{32,33},{3... | collective-permute-start | bytes 7864328 | tf_op jit(solution)/shard_map/ppermute | solution.py:37
  188.9 25.3 %collective-permute-start.18 = (bf16[2,192,1280]{2,1,0:T(8,128)(2,1)S(1)}, bf16[2,192,1280]{2,1,0:T(8,128)(2,1)S(1)}, u32[]{:S(2)}, u32[]{:S(2)}) collective-permute-start(bf16[2,192,1280]{2,1,0:T(8,128)(2,1)S(1)} %collective-permute-done.17), channel_id=1, source_target_pairs={{0,1},{1,0},{8,9},{9,8},{16,17},{17,16},{24,25},{25,24},{32,33},{3... | collective-permute-start | bytes 2949128 | tf_op jit(solution)/shard_map/ppermute | solution.py:37
  192.2 15.2 %collective-permute-start.19 = (bf16[2,192,1280]{2,1,0:T(8,128)(2,1)S(1)}, bf16[2,192,1280]{2,1,0:T(8,128)(2,1)}, u32[]{:S(2)}, u32[]{:S(2)}) collective-permute-start(bf16[2,192,1280]{2,1,0:T(8,128)(2,1)S(1)} %collective-permute-done.17), channel_id=1, source_target_pairs={{0,2},{1,391},{8,10},{9,399},{16,18},{17,407},{24,26},{25,415},{32... | collective-permute-start | bytes 2949128 | tf_op jit(solution)/shard_map/ppermute | solution.py:37
  207.4 28.7 %collective-permute-start.20 = (bf16[2,192,1280]{2,1,0:T(8,128)(2,1)}, bf16[2,192,1280]{2,1,0:T(8,128)(2,1)}, u32[]{:S(2)}, u32[]{:S(2)}) collective-permute-start(bf16[2,192,1280]{2,1,0:T(8,128)(2,1)} %collective-permute-done.19), channel_id=1, source_target_pairs={{0,1},{1,0},{8,9},{9,8},{16,17},{17,16},{24,25},{25,24},{32,33},{3... | collective-permute-start | bytes 2949128 | tf_op jit(solution)/shard_map/ppermute | solution.py:37
  211.4 18.8 %collective-permute-start.21 = (bf16[2,192,1280]{2,1,0:T(8,128)(2,1)}, bf16[2,192,1280]{2,1,0:T(8,128)(2,1)}, u32[]{:S(2)}, u32[]{:S(2)}) collective-permute-start(bf16[2,192,1280]{2,1,0:T(8,128)(2,1)} %collective-permute-done.19), channel_id=1, source_target_pairs={{0,2},{1,391},{8,10},{9,399},{16,18},{17,407},{24,26},{25,415},{32... | collective-permute-start | bytes 2949128 | tf_op jit(solution)/shard_map/ppermute | solution.py:37
  217.5 3.0 copy-start.5
  220.5 3.5 copy-start.2
  220.5 3.5 copy-start.6
  226.5 78.5 %all-to-all-start.1 = ((bf16[16,64,1280]{2,1,0:T(8,128)(2,1)}), bf16[16,64,1280]{2,1,0:T(8,128)(2,1)S(1)}, u32[]{:S(2)}, u32[]{:S(2)}) async-start(bf16[16,64,1280]{2,1,0:T(8,128)(2,1)} %bitcast.112), calls=%async_computation.1 | async-start | bytes 5242880 | tf_op jit(solution)/shard_map/all_to_all | solution.py:224
  230.2 24.3 %collective-permute-start.22 = (bf16[2,192,1280]{2,1,0:T(8,128)(2,1)}, bf16[2,192,1280]{2,1,0:T(8,128)(2,1)S(1)}, u32[]{:S(2)}, u32[]{:S(2)}) collective-permute-start(bf16[2,192,1280]{2,1,0:T(8,128)(2,1)} %collective-permute-done.21), channel_id=1, source_target_pairs={{0,1},{1,0},{8,9},{9,8},{16,17},{17,16},{24,25},{25,24},{32,33},{3... | collective-permute-start | bytes 2949128 | tf_op jit(solution)/shard_map/ppermute | solution.py:37
  232.1 15.3 %collective-permute-start.23 = (bf16[2,192,1280]{2,1,0:T(8,128)(2,1)}, bf16[2,192,1280]{2,1,0:T(8,128)(2,1)S(1)}, u32[]{:S(2)}, u32[]{:S(2)}) collective-permute-start(bf16[2,192,1280]{2,1,0:T(8,128)(2,1)} %collective-permute-done.21), channel_id=1, source_target_pairs={{0,2},{1,391},{8,10},{9,399},{16,18},{17,407},{24,26},{25,415},{32... | collective-permute-start | bytes 2949128 | tf_op jit(solution)/shard_map/ppermute | solution.py:37
  247.5 25.7 %collective-permute-start.24 = (bf16[2,192,1280]{2,1,0:T(8,128)(2,1)S(1)}, bf16[2,192,1280]{2,1,0:T(8,128)(2,1)S(1)}, u32[]{:S(2)}, u32[]{:S(2)}) collective-permute-start(bf16[2,192,1280]{2,1,0:T(8,128)(2,1)S(1)} %collective-permute-done.23), channel_id=1, source_target_pairs={{0,1},{1,0},{8,9},{9,8},{16,17},{17,16},{24,25},{25,24},{32,33},{3... | collective-permute-start | bytes 2949128 | tf_op jit(solution)/shard_map/ppermute | solution.py:37
  251.9 15.1 %collective-permute-start.25 = (bf16[2,192,1280]{2,1,0:T(8,128)(2,1)S(1)}, bf16[2,192,1280]{2,1,0:T(8,128)(2,1)S(1)}, u32[]{:S(2)}, u32[]{:S(2)}) collective-permute-start(bf16[2,192,1280]{2,1,0:T(8,128)(2,1)S(1)} %collective-permute-done.23), channel_id=1, source_target_pairs={{0,2},{1,391},{8,10},{9,399},{16,18},{17,407},{24,26},{25,415},{32... | collective-permute-start | bytes 2949128 | tf_op jit(solution)/shard_map/ppermute | solution.py:37
  267.1 8.2 %collective-permute-start.26 = (bf16[2,192,1280]{2,1,0:T(8,128)(2,1)S(1)}, bf16[2,192,1280]{2,1,0:T(8,128)(2,1)S(1)}, u32[]{:S(2)}, u32[]{:S(2)}) collective-permute-start(bf16[2,192,1280]{2,1,0:T(8,128)(2,1)S(1)} %collective-permute-done.25), channel_id=1, source_target_pairs={{0,1},{1,0},{8,9},{9,8},{16,17},{17,16},{24,25},{25,24},{32,33},{3... | collective-permute-start | bytes 2949128 | tf_op jit(solution)/shard_map/ppermute | solution.py:37
  271.2 15.2 %collective-permute-start.27 = (bf16[2,192,1280]{2,1,0:T(8,128)(2,1)S(1)}, bf16[2,192,1280]{2,1,0:T(8,128)(2,1)}, u32[]{:S(2)}, u32[]{:S(2)}) collective-permute-start(bf16[2,192,1280]{2,1,0:T(8,128)(2,1)S(1)} %collective-permute-done.25), channel_id=1, source_target_pairs={{0,2},{1,391},{8,10},{9,399},{16,18},{17,407},{24,26},{25,415},{32... | collective-permute-start | bytes 2949128 | tf_op jit(solution)/shard_map/ppermute | solution.py:37
  288.9 10.0 %collective-permute-start.29 = (bf16[1,192,1280]{2,1,0:T(8,128)(2,1)S(1)}, bf16[1,192,1280]{2,1,0:T(8,128)(2,1)}, u32[]{:S(2)}, u32[]{:S(2)}) collective-permute-start(bf16[1,192,1280]{2,1,0:T(8,128)(2,1)S(1)} %get-tuple-element.16), channel_id=1, source_target_pairs={{0,2},{1,391},{8,10},{9,399},{16,18},{17,407},{24,26},{25,415},{32... | collective-permute-start | bytes 1474568 | tf_op jit(solution)/shard_map/ppermute | solution.py:37
  291.7 16.8 %collective-permute-start.28 = (bf16[2,192,1280]{2,1,0:T(8,128)(2,1)}, bf16[2,192,1280]{2,1,0:T(8,128)(2,1)}, u32[]{:S(2)}, u32[]{:S(2)}) collective-permute-start(bf16[2,192,1280]{2,1,0:T(8,128)(2,1)} %collective-permute-done.27), channel_id=1, source_target_pairs={{0,1},{1,0},{8,9},{9,8},{16,17},{17,16},{24,25},{25,24},{32,33},{3... | collective-permute-start | bytes 2949128 | tf_op jit(solution)/shard_map/ppermute | solution.py:37
  298.8 7.9 %collective-permute-start.30 = (bf16[1,192,1280]{2,1,0:T(8,128)(2,1)}, bf16[1,192,1280]{2,1,0:T(8,128)(2,1)}, u32[]{:S(2)}, u32[]{:S(2)}) collective-permute-start(bf16[1,192,1280]{2,1,0:T(8,128)(2,1)} %collective-permute-done.29), channel_id=1, source_target_pairs={{0,1},{1,0},{8,9},{9,8},{16,17},{17,16},{24,25},{25,24},{32,33},{3... | collective-permute-start | bytes 1474568 | tf_op jit(solution)/shard_map/ppermute | solution.py:37
  306.7 5.1 %copy-start.1 = (bf16[16,4,16,1280]{3,2,0,1:T(8,128)(2,1)S(1)}, bf16[16,4,16,1280]{3,2,0,1:T(8,128)(2,1)}, u32[]{:S(2)}) copy-start(bf16[16,4,16,1280]{3,2,0,1:T(8,128)(2,1)} %copy.51) | copy-start | bytes 7864324
  323.1 10.1 %copy-start.7 = (f32[128,6]{0,1:T(8,128)S(1)}, f32[128,6]{0,1:T(8,128)}, u32[]{:S(2)}) copy-start(f32[128,6]{0,1:T(8,128)} %param.19) | copy-start | bytes 9220
  326.6 41.3 %all-to-all-start.2 = ((bf16[16,64,1280]{2,1,0:T(8,128)(2,1)}), bf16[16,64,1280]{2,1,0:T(8,128)(2,1)S(1)}, u32[]{:S(2)}, u32[]{:S(2)}) async-start(bf16[16,64,1280]{2,1,0:T(8,128)(2,1)} %bitcast.113), calls=%async_computation.2 | async-start | bytes 5242880 | tf_op jit(solution)/shard_map/all_to_all | solution.py:241

commit v2 on v0

v2 whole, which is shorter than its diff:
```python
import math
import jax
import jax.numpy as jnp
from jax import lax
from jax.experimental import pallas as pl
from jax.experimental.pallas import tpu as pltpu
from jax.sharding import PartitionSpec as P

HEAD = 128
TOP = 6
CAP = 16
MESH = pl.DeviceIdType.MESH
ZH, NX, NY, ZL, NC = 4, 4, 4, 4, 2
NZ = ZH * ZL
PLANE = NX * NY
N_CTX = ZH * PLANE


def fetch_and_attend(queries, keys, values, segment_ids, out_proj, expert_up, expert_down):
    shard_len, width = queries.shape
    block_rows = min(256, shard_len)
    span = shard_len + block_rows
    tiles = shard_len // block_rows
    scale = HEAD ** (-0.5) * math.log2(math.e)
    units, features = expert_up.shape[1:]
    rows = out_proj.shape[0] // PLANE
    last = NZ // 2

    def kernel(
        q_ref, k_ref, v_ref, mq_ref, seg_ref, proj_ref, up_ref, down_ref,
        att_ref, whole_ref, experts_ref,
        k2, v2, m2, ring_s, ring_r, swap_s, swap_r, send_s, recv_s, local_s,
    ):
        ctx, exp = lax.axis_index("ctx"), lax.axis_index("exp")
        zh, x, y = ctx // PLANE, (ctx // NY) % NX, ctx % NY
        zl, c = exp // NC, exp % NC
        z, p = zh * ZL + zl, ctx % PLANE

        def device(z, x, y, c):
            return ((z // ZL) * PLANE + x * NY + y, (z % ZL) * NC + c)

        def piece(step):
            return (z + (2 * c - 1) * step + 2 * NZ) % NZ

        partner = device(z, x, y, 1 - c)
        ahead = device((z + 1 - 2 * c + NZ) % NZ, x, y, c)
        behind = device((z + 2 * c - 1 + NZ) % NZ, x, y, c)
        line = [device(zh * ZL + (zl + d) % ZL, x, y, c) for d in (1, 2, 3)]
        column = [device(z, x, (y + d) % NY, c) for d in (1, 2, 3)]
        right, left = device(z, (x + 1) % NX, y, c), device(z, (x + 3) % NX, y, c)
        after, before = ((ctx + 1) % N_CTX, exp), ((ctx + N_CTX - 1) % N_CTX, exp)
        greeted = [partner, ahead, behind, *line, *column, right, left, after, before]
        barrier = pltpu.get_barrier_semaphore()
        for other in greeted:
            pl.semaphore_signal(barrier, inc=1, device_id=other, device_id_type=MESH)
        pl.semaphore_wait(barrier, len(greeted))

        def remote(src, dst, sent, received, target):
            return pltpu.make_async_remote_copy(
                src_ref=src, dst_ref=dst, send_sem=sent, recv_sem=received,
                device_id=target, device_id_type=MESH,
            )

        def other(src, dst, index, target):
            return remote(src, dst, send_s.at[index], recv_s.at[index], target)

        def ring_at(index, which, at):
            slot = experts_ref.at[which, at]
            return remote(slot, slot, ring_s.at[index], ring_r.at[index], ahead)

        def swap_at(index, which, at):
            slot = experts_ref.at[which, at]
            return remote(slot, slot, swap_s.at[index], swap_r.at[index], partner)

        locals_ = []
        pairs = []
        for which, ref in enumerate((up_ref, down_ref)):
            slot = experts_ref.at[which, z, c]
            pairs.append(other(ref.at[0], slot, which, partner))
            locals_.append(pltpu.make_async_copy(ref.at[0], slot, local_s.at[which]))
        for copy in pairs + locals_:
            copy.start()
        early = pl.ds(0, shard_len)
        late = pl.ds(shard_len, shard_len)
        shift = [
            other(k_ref, k2.at[early], 2, after),
            other(v_ref, v2.at[early], 3, after),
            other(seg_ref, m2.at[:, early], 4, after),
        ]
        stay = [
            pltpu.make_async_copy(k_ref, k2.at[late], local_s.at[2]),
            pltpu.make_async_copy(v_ref, v2.at[late], local_s.at[3]),
            pltpu.make_async_copy(seg_ref, m2.at[:, late], local_s.at[4]),
        ]
        rows_own = whole_ref.at[zl, c, p]
        proj_own = pltpu.make_async_copy(proj_ref.at[p], rows_own, local_s.at[5])
        along_z = [other(proj_ref.at[p], rows_own, 5 + d, line[d]) for d in range(3)]
        for copy in along_z + shift + stay + [proj_own]:
            copy.start()
        for copy in pairs:
            copy.wait()
        for copy in locals_:
            copy.wait()
        for which in range(2):
            first = ring_at(which, which, z)
            first.start()

        def service(n, step, which):
            at = piece(step)
            ring_at(n, which, at).wait_recv()
            swap_at(n, which, at).start()
            return at

        def forward(n, step, which):
            at = service(n, step, which)
            ring_at(n + 2, which, at).start()

        block_y = whole_ref.at[:, c, p]
        along_y = [other(block_y, block_y, 8 + d, column[d]) for d in range(3)]

        def x_block(at):
            return whole_ref.at[:, c, pl.ds(at * NY, NY)]

        along_x = [
            other(x_block(x), x_block(x), 11, right),
            other(x_block(x), x_block(x), 12, left),
        ]
        from_left = whole_ref.at[pl.ds(0, 2), c, pl.ds((x + 3) % NX * NY, NY)]
        from_right = whole_ref.at[pl.ds(2, 2), c, pl.ds((x + 1) % NX * NY, NY)]
        opposite = [
            other(from_left, from_left, 13, right),
            other(from_right, from_right, 14, left),
        ]
        core_half = whole_ref.at[:, c]
        crossing = other(core_half, core_half, 15, partner)

        for copy in along_z:
            copy.wait_recv()
        proj_own.wait()
        for copy in along_y:
            copy.start()
        forward(0, 1, 0)
        for copy in along_y:
            copy.wait_recv()
        for copy in along_x:
            copy.start()
        forward(1, 1, 1)
        forward(2, 2, 0)
        forward(3, 2, 1)
        for copy in stay:
            copy.wait()
        for copy in shift:
            copy.wait_recv()
        for copy in along_x:
            copy.wait_recv()
        for copy in opposite:
            copy.start()
        column_at = lax.broadcasted_iota(jnp.int32, (block_rows, span), 1)
        row_at = lax.broadcasted_iota(jnp.int32, (block_rows, span), 0)

        def one_tile(tile):
            head = pl.ds(pl.multiple_of(tile // tiles * HEAD, HEAD), HEAD)
            start = pl.multiple_of(tile % tiles * block_rows, block_rows)
            window = pl.ds(start, span)
            here = pl.ds(start, block_rows)
            scores = lax.dot_general(
                q_ref[here, head], k2[window, head], (((1,), (1,)), ((), ())),
                preferred_element_type=jnp.float32,
            )
            least = jnp.where(ctx == 0, shard_len - start, 0)
            allowed = (m2[:, window] == mq_ref[here, :]) & (column_at - row_at <= shard_len)
            allowed = allowed & (column_at >= least)
            scores = jnp.where(allowed, scores, -1e30)
            row_max = jnp.max(scores, axis=1, keepdims=True)
            weights = jnp.exp2((scores - row_max) * scale)
            total = jnp.sum(weights, axis=1, keepdims=True)
            mixed = jnp.dot(
                weights.astype(jnp.bfloat16), v2[window, head], preferred_element_type=jnp.float32
            )
            att_ref[here, head] = (mixed / total).astype(att_ref.dtype)

        per_turn = tiles * (width // HEAD) // 4

        def turn(n, carry):
            forward(n, n // 2 + 1, n % 2)

            def inner(i, carry):
                one_tile((n - 4) * per_turn + i)
                return carry

            return lax.fori_loop(0, per_turn, inner, carry)

        lax.fori_loop(4, 8, turn, 0)
        for copy in opposite:
            copy.wait_recv()
        crossing.start()
        for n in range(8, 12):
            forward(n, n // 2 + 1, n % 2)
        for which in range(2):
            service(12 + which, last - 1, which)
        ring_at(14, c, piece(last - 1)).start()
        service(14, last, c)
        for copy in along_z + along_y + along_x + opposite + shift:
            copy.wait_send()
        crossing.wait()
        for n in range(14):
            at = z
            ring_at(n, n % 2, at).wait_send()
            swap_at(n, n % 2, at).wait()
        ring_at(14, c, z).wait_send()
        swap_at(14, c, z).wait()

    anywhere = pl.BlockSpec(memory_space=pl.ANY)
    vmem = pl.BlockSpec(memory_space=pltpu.VMEM)
    return pl.pallas_call(
        kernel,
        in_specs=[vmem, anywhere, anywhere, vmem, vmem, anywhere, vmem, vmem],
        out_specs=[vmem, anywhere, anywhere],
        out_shape=[
            jax.ShapeDtypeStruct(queries.shape, queries.dtype),
            jax.ShapeDtypeStruct((ZL, NC, PLANE, rows, features), out_proj.dtype),
            jax.ShapeDtypeStruct((2, NZ, NC, units, features), expert_up.dtype),
        ],
        scratch_shapes=[
            pltpu.VMEM((2 * shard_len, width), keys.dtype),
            pltpu.VMEM((2 * shard_len, width), values.dtype),
            pltpu.VMEM((1, 2 * shard_len), jnp.int32),
            pltpu.SemaphoreType.DMA((15,)),
            pltpu.SemaphoreType.DMA((15,)),
            pltpu.SemaphoreType.DMA((15,)),
            pltpu.SemaphoreType.DMA((15,)),
            pltpu.SemaphoreType.DMA((16,)),
            pltpu.SemaphoreType.DMA((16,)),
            pltpu.SemaphoreType.DMA((6,)),
        ],
        compiler_params=pltpu.CompilerParams(
            collective_id=0, has_side_effects=True, vmem_limit_bytes=40 * 2**20
        ),
        name="fetch_and_attend",
    )(
        queries, keys, values, segment_ids[:, None], segment_ids[None, :],
        out_proj.reshape(PLANE, rows, features), expert_up, expert_down,
    )


def run_experts(arrived, experts):
    sources, count, slots, features = arrived.shape

    def kernel(x_ref, up_ref, down_ref, out_ref):
        tokens = x_ref[...].reshape(sources * slots, features)
        up = up_ref[...].reshape(-1, features)
        down = down_ref[...].reshape(-1, features)
        hidden = lax.dot_general(
            tokens, up, (((1,), (1,)), ((), ())), preferred_element_type=jnp.float32
        )
        hidden = (hidden / (1.0 + jnp.exp(-hidden))).astype(jnp.bfloat16)
        result = jnp.dot(hidden, down, preferred_element_type=jnp.float32)
        out_ref[...] = result.astype(out_ref.dtype).reshape(out_ref.shape)

    block = (sources, 1, slots, features)
    weights = (1, ZL) + experts.shape[2:]
    return pl.pallas_call(
        kernel,
        grid=(count,),
        in_specs=[
            pl.BlockSpec(block, lambda h: (0, h, 0, 0)),
            pl.BlockSpec(weights, lambda h: (0, h, 0, 0, 0)),
            pl.BlockSpec(weights, lambda h: (1, h, 0, 0, 0)),
        ],
        out_specs=pl.BlockSpec(block, lambda h: (0, h, 0, 0)),
        out_shape=jax.ShapeDtypeStruct(arrived.shape, arrived.dtype),
        name="run_experts",
    )(arrived, experts, experts)


def shards(
    queries,
    keys,
    values,
    segment_ids,
    out_proj,
    residual,
    norm_gain,
    expert_ids,
    gate_weights,
    expert_up,
    expert_down,
):
    shard_len = queries.shape[0]
    heads_here = queries.shape[1] // HEAD
    attention, out_whole, experts_here = fetch_and_attend(
        queries, keys, values, segment_ids, out_proj, expert_up, expert_down
    )
    groups = lax.axis_size("exp")
    tok_rows = shard_len // groups
    mine = lax.all_to_all(
        attention.reshape(groups, tok_rows, heads_here * HEAD), "exp", 0, 0, tiled=True
    )
    projected = jnp.einsum(
        "etk,ekd->td",
        mine,
        out_whole.reshape(groups, heads_here * HEAD, -1),
        preferred_element_type=jnp.float32,
    )
    stream = (residual.astype(jnp.float32) + projected).astype(jnp.bfloat16)
    stream_f = stream.astype(jnp.float32)
    mean_square = jnp.mean(stream_f * stream_f, axis=1, keepdims=True)
    normed = (stream_f * lax.rsqrt(mean_square + 1e-06) * norm_gain[None, :]).astype(jnp.bfloat16)
    feature_count = stream.shape[1]
    experts = lax.axis_size("ctx")
    slots = experts * CAP
    flat_ids = expert_ids.reshape(-1)
    one_hot = (flat_ids[:, None] == jnp.arange(experts, dtype=jnp.int32)[None, :]).astype(jnp.int32)
    earlier = jnp.cumsum(one_hot, axis=0) - one_hot
    slot_rank = jnp.sum(earlier * one_hot, axis=1)
    place = flat_ids % PLANE * ZH + flat_ids // PLANE
    slot_grid = (place * CAP + slot_rank).reshape(tok_rows, TOP)
    hits = slot_grid[:, :, None] == jnp.arange(slots, dtype=jnp.int32)[None, None, :]
    placing = jnp.any(hits, axis=1).astype(jnp.bfloat16)
    gates = jnp.sum(jnp.where(hits, gate_weights[:, :, None], 0.0), axis=1)
    gates_high = gates.astype(jnp.bfloat16)
    gates_low = (gates - gates_high.astype(jnp.float32)).astype(jnp.bfloat16)
    outgoing = lax.dot_general(
        placing, normed, (((0,), (0,)), ((), ())), preferred_element_type=jnp.float32
    ).astype(jnp.bfloat16)
    plane_groups = [[h * PLANE + p for p in range(PLANE)] for h in range(ZH)]
    arrived = lax.all_to_all(
        outgoing.reshape(PLANE, ZH * CAP, feature_count),
        "ctx",
        0,
        0,
        axis_index_groups=plane_groups,
        tiled=True,
    )
    result = run_experts(arrived.reshape(PLANE, ZH, CAP, feature_count), experts_here)
    returned = lax.all_to_all(
        result.reshape(PLANE, ZH * CAP, feature_count),
        "ctx",
        0,
        0,
        axis_index_groups=plane_groups,
        tiled=True,
    ).reshape(slots, feature_count)
    mixture = jnp.dot(gates_high, returned, preferred_element_type=jnp.float32) + jnp.dot(
        gates_low, returned, preferred_element_type=jnp.float32
    )
    return (stream_f + mixture).astype(jnp.bfloat16)


def solution(mesh):
    in_specs = (
        P("ctx", "exp"),
        P("ctx", "exp"),
        P("ctx", "exp"),
        P("ctx"),
        P("exp", None),
        P(("ctx", "exp"), None),
        P(),
        P(("ctx", "exp"), None),
        P(("ctx", "exp"), None),
        P("ctx", "exp", None),
        P("ctx", "exp", None),
    )
    out_specs = P(("ctx", "exp"), None)
    return jax.shard_map(shards, mesh=mesh, in_specs=in_specs, out_specs=out_specs, check_vma=False)
```

time: 557 us -> 315 us (0.57)
  waiting for transfers between devices: 431 us -> 40.5 us
  Pallas kernels: 0 us -> 180 us
  blocking collectives: 0 us -> 60.8 us
  starting transfers between devices: 43.5 us -> 7.93 us
  matrix products: 28.7 us -> 7.27 us
  other arithmetic: 17.2 us -> 3.77 us
  between operations: 13.4 us -> 0.15 us
  local copies, waits for them, and re-layouts: 18.8 us -> 10.8 us
    pallas_call x0 -> x2, Pallas kernels: none -> 180 us  [the longest x1 169 us: fetch_and_attend(): pl.pallas_call(kernel, in_specs=[vmem, anywhere, anywhere, vmem, vmem, an...]
    all_gather x2 -> x0, waiting for transfers between devices: 173 us -> none  [the longest x1 110 us: shards(): lax.all_gather(expert_up, 'exp', axis=1, tiled=True)]
    reduce_scatter x1 -> x0, waiting for transfers between devices: 120 us -> none  [shards(): lax.psum_scatter(jnp.dot(row_block, out_proj, preferred_element_type=jnp....]
    all_to_all x2, waiting for transfers between devices: 122 us -> 40.5 us  [the longest x1 29.6 us: shards(): lax.all_to_all(result.reshape(PLANE, ZH * CAP, feature_count), 'ctx', 0,...]
    all_to_all x0 -> x1, blocking collectives: none -> 60.8 us  [shards(): lax.all_to_all(outgoing.reshape(PLANE, ZH * CAP, feature_count), 'ctx', 0...]
    all_to_all x2, starting transfers between devices: 33 us -> 7.93 us  [the longest x1 4.07 us: shards(): lax.all_to_all(attention.reshape(groups, tok_rows, heads_here * HEAD), 'e...]
    dot_general x11 -> x4, matrix products: 28.7 us -> 7.27 us  [the longest x1 3.43 us: shards(): jnp.einsum('etk,ekd->td', mine, out_whole.reshape(groups, heads_here * HE...]
    ppermute x3 -> x0, waiting for transfers between devices: 14 us -> none  [shifted(): return lax.ppermute(block, axis, route)]
  transfers between devices with their start and end apart: 8 -> 2, of which waited for: 6 -> 2; matrix products, arithmetic and copies ran while one was open for 1% -> 1% of each run, Pallas kernels for 0% -> 0%
where the time goes in v2:
time: 315 us; the launch traced here: 311 us
  Pallas kernels  180 us (57%)
  blocking collectives  60.8 us (19%)
  waiting for transfers between devices  40.5 us (13%)
  local copies, waits for them, and re-layouts  10.8 us (3%)
  starting transfers between devices  7.93 us (3%)
  matrix products  7.27 us (2%)
  other arithmetic  3.77 us (1%)
    pallas_call x1, Pallas kernels, fetch_and_attend(): pl.pallas_call(kernel, in_specs=[vmem, anywhere, anywhere, vmem, vmem, an...  169 us
    all_to_all x1, blocking collectives, shards(): lax.all_to_all(outgoing.reshape(PLANE, ZH * CAP, feature_count), 'ctx', 0...  60.8 us
    all_to_all x1, waiting for transfers between devices, shards(): lax.all_to_all(result.reshape(PLANE, ZH * CAP, feature_count), 'ctx', 0,...  29.6 us
    all_to_all x1, waiting for transfers between devices, shards(): lax.all_to_all(attention.reshape(groups, tok_rows, heads_here * HEAD), 'e...  10.9 us
    pallas_call x1, Pallas kernels, run_experts(): pl.pallas_call(kernel, grid=(count,), in_specs=[pl.BlockSpec(block, lambd...  10.3 us
    unnamed x27, local copies, waits for them, and re-layouts  9.15 us
  transfers between devices with their start and end apart: 2, of which 2 were waited for; matrix products, arithmetic and copies ran while one was open for 1% of the time, Pallas kernels for 0%

profile of v2, /device:TPU:1, one launch (start us, length us, event | category | flops | bytes accessed | tf_op | source)
XLA Modules:
  0.0 310.9 jit_solution(3339372326933357254)
XLA Ops:
  0.0 0.0 copy-start.12
  0.0 0.0 copy-start.9
  0.0 0.9 copy.23.mq_ref
  1.0 0.0 copy-start.1
  1.0 1.1 copy-done.1
  2.1 0.0 copy-start.2
  2.1 1.0 copy-done.2
  3.1 1.0 copy-done.3
  4.1 0.0 copy-start.4
  4.1 1.0 copy-done.4
  5.2 0.0 copy-start.5
  5.2 0.9 copy-done.5
  6.1 0.0 copy-start.6
  6.1 0.9 copy-done.6
  7.1 0.0 copy-start.7
  7.1 0.7 copy-done.7
  7.8 169.4 %fetch_and_attend.1 = (bf16[1024,256]{1,0:T(8,128)(2,1)}, bf16[4,2,16,16,1280]{4,3,2,1,0:T(8,128)(2,1)S(1)}, bf16[2,16,2,96,1280]{4,3,2,1,0:T(8,128)(2,1)}) custom-call(bf16[1024,256]{1,0:T(8,128)(2,1)S(1)} %copy-done.2, bf16[1024,256]{1,0:T(8,128)(2,1)S(1)} %copy-done.3, bf16[1024,256]{1,0:T(8,128)(2,1)S(1)} %copy-done.4, s32[1024,1]{1,0:T(8,128)S(1)} %copy.23.mq_ref, ...), custom_call_target="tpu_custom_call" | custom-call | tf_op jit(solution)/shard_map/fetch_and_attend/pallas_call | solution.py:215
  177.1 0.0 copy-start
  177.2 2.2 copy-done
  179.4 4.1 %all-to-all-start = ((bf16[8,128,256]{2,1,0:T(8,128)(2,1)}), bf16[8,128,256]{2,1,0:T(8,128)(2,1)S(1)}, u32[]{:S(2)}, u32[]{:S(2)}) async-start(bf16[8,128,256]{2,1,0:T(8,128)(2,1)} %bitcast.3), calls=%async_computation | async-start | bytes 1048576 | tf_op jit(solution)/shard_map/all_to_all | solution.py:296
  183.5 0.0 copy-done.12
  183.5 0.1 copy.24
  183.6 0.1 eq.40
  183.7 0.1 eq.44
  183.9 1.8 reduce-window.6
  185.7 0.3 slice_reduce_fusion
  186.0 0.1 fusion.10
  186.1 0.1 reduce_sum.30
  186.3 0.1 fusion.18
  186.3 0.1 copy.31
  186.4 0.5 fusion
  186.9 10.9 %all-to-all-done = bf16[8,128,256]{2,1,0:T(8,128)(2,1)S(1)} async-done(((bf16[8,128,256]{2,1,0:T(8,128)(2,1)}), bf16[8,128,256]{2,1,0:T(8,128)(2,1)S(1)}, u32[]{:S(2)}, u32[]{:S(2)}) %all-to-all-start) | async-done | bytes 524320 | tf_op jit(solution)/shard_map/all_to_all | solution.py:296
  197.8 0.0 copy-done.9
  197.8 0.0 copy-start.10
  197.8 3.4 %multiply_reduce_fusion = (f32[128]{0:T(128)S(1)}, f32[128,1280]{1,0:T(8,128)S(1)}) fusion(bf16[8,128,256]{2,1,0:T(8,128)(2,1)S(1)} %all-to-all-done, bf16[8,256,1280]{2,1,0:T(8,128)(2,1)} %bitcast.42, bf16[128,1280]{1,0:T(8,128)(2,1)S(1)} %copy-done.9), kind=kOutput, calls=%fused_computation.12 | convolution fusion | flops 672071552 | bytes 6750720 | tf_op jit(solution)/shard_map/etk,ekd->td/dot_general | solution.py:299
  201.3 0.0 copy-done.10
  201.3 0.9 convolution_convert_fusion
  202.2 60.8 %all_to_all.15 = bf16[16,64,1280]{2,1,0:T(8,128)(2,1)} all-to-all(bf16[16,64,1280]{2,1,0:T(8,128)(2,1)S(1)} %bitcast.50), channel_id=1, replica_groups={{0,8,16,24,32,40,48,56,64,72,80,88,96,104,112,120},{128,136,144,152,160..., dimensions={0} | all-to-all | bytes 5242880 | tf_op jit(solution)/shard_map/all_to_all | solution.py:327
  263.0 10.3 %run_experts.1 = bf16[16,4,16,1280]{3,2,1,0:T(8,128)(2,1)} custom-call(bf16[16,4,16,1280]{3,2,1,0:T(8,128)(2,1)} %bitcast.49, bf16[2,16,2,96,1280]{4,3,2,1,0:T(8,128)(2,1)} %get-tuple-element.10.up_ref.down_ref, bf16[2,16,2,96,1280]{4,3,2,1,0:T(8,128)(2,1)} %get-tuple-element.10.up_ref.down_ref), custom_call_target="tpu_custom_call" | custom-call | tf_op jit(solution)/shard_map/run_experts/pallas_call | solution.py:262
  273.3 0.0 copy-start.11
  273.3 3.9 %all-to-all-start.2 = ((bf16[16,64,1280]{2,1,0:T(8,128)(2,1)}), bf16[16,64,1280]{2,1,0:T(8,128)(2,1)S(1)}, u32[]{:S(2)}, u32[]{:S(2)}) async-start(bf16[16,64,1280]{2,1,0:T(8,128)(2,1)} %bitcast.48), calls=%async_computation.2 | async-start | bytes 5242880 | tf_op jit(solution)/shard_map/all_to_all | solution.py:336
  277.2 0.0 copy-done.11
  277.2 1.2 select_reduce_fusion
  278.4 29.6 %all-to-all-done.2 = bf16[16,64,1280]{2,1,0:T(8,128)(2,1)S(1)} async-done(((bf16[16,64,1280]{2,1,0:T(8,128)(2,1)}), bf16[16,64,1280]{2,1,0:T(8,128)(2,1)S(1)}, u32[]{:S(2)}, u32[]{:S(2)}) %all-to-all-start.2) | async-done | bytes 2621472 | tf_op jit(solution)/shard_map/all_to_all | solution.py:336
  308.0 0.0 copy-start.8
  308.0 1.6 fusion.13
  309.6 0.0 copy-done.8
  309.6 1.3 fusion.3
  (4 shorter events, 0.1 us)
Async XLA Ops:
  0.0 183.5 %copy-start.12 = (s32[128,6]{0,1:T(8,128)S(1)}, s32[128,6]{0,1:T(8,128)}, u32[]{:S(2)}) copy-start(s32[128,6]{0,1:T(8,128)} %param.18) | copy-start | bytes 9220
  0.0 197.8 %copy-start.9 = (bf16[128,1280]{1,0:T(8,128)(2,1)S(1)}, bf16[128,1280]{1,0:T(8,128)(2,1)}, u32[]{:S(2)}) copy-start(bf16[128,1280]{1,0:T(8,128)(2,1)} %param.16) | copy-start | bytes 983044
  1.0 1.1 copy-start.1
  2.1 1.0 copy-start.2
  3.1 1.0 copy-start.3
  4.1 1.0 copy-start.4
  5.2 0.9 copy-start.5
  6.1 0.9 copy-start.6
  7.1 0.7 copy-start.7
  177.1 2.2 copy-start
  179.4 18.4 %all-to-all-start = ((bf16[8,128,256]{2,1,0:T(8,128)(2,1)}), bf16[8,128,256]{2,1,0:T(8,128)(2,1)S(1)}, u32[]{:S(2)}, u32[]{:S(2)}) async-start(bf16[8,128,256]{2,1,0:T(8,128)(2,1)} %bitcast.3), calls=%async_computation | async-start | bytes 1048576 | tf_op jit(solution)/shard_map/all_to_all | solution.py:296
  197.8 3.5 %copy-start.10 = (f32[1280]{0:T(1024)S(1)}, f32[1280]{0:T(1024)}, u32[]{:S(2)}) copy-start(f32[1280]{0:T(1024)} %param.17) | copy-start | bytes 15364
  273.3 3.9 %copy-start.11 = (f32[128,6]{0,1:T(8,128)S(1)}, f32[128,6]{0,1:T(8,128)}, u32[]{:S(2)}) copy-start(f32[128,6]{0,1:T(8,128)} %param.19) | copy-start | bytes 9220
  273.3 34.7 %all-to-all-start.2 = ((bf16[16,64,1280]{2,1,0:T(8,128)(2,1)}), bf16[16,64,1280]{2,1,0:T(8,128)(2,1)S(1)}, u32[]{:S(2)}, u32[]{:S(2)}) async-start(bf16[16,64,1280]{2,1,0:T(8,128)(2,1)} %bitcast.48), calls=%async_computation.2 | async-start | bytes 5242880 | tf_op jit(solution)/shard_map/all_to_all | solution.py:336
  308.0 1.6 copy-start.8

commit v3 on v2

--- a/solution.py
+++ b/solution.py
@@ -16,6 +16,102 @@
 N_CTX = ZH * PLANE
 
 
+def place():
+    ctx, exp = lax.axis_index("ctx"), lax.axis_index("exp")
+    zh, x, y = ctx // PLANE, (ctx // NY) % NX, ctx % NY
+    zl, c = exp // NC, exp % NC
+    return zh * ZL + zl, x, y, c
+
+
+def device(z, x, y, c):
+    return ((z // ZL) * PLANE + x * NY + y, (z % ZL) * NC + c)
+
+
+def greet(others):
+    barrier = pltpu.get_barrier_semaphore()
+    for other in others:
+        pl.semaphore_signal(barrier, inc=1, device_id=other, device_id_type=MESH)
+    pl.semaphore_wait(barrier, len(others))
+
+
+def remote(src, dst, sent, received, target):
+    return pltpu.make_async_remote_copy(
+        src_ref=src, dst_ref=dst, send_sem=sent, recv_sem=received,
+        device_id=target, device_id_type=MESH,
+    )
+
+
+def column_ring(experts_ref, ring_s, ring_r, swap_s, swap_r):
+    z, x, y, c = place()
+    partner = device(z, x, y, 1 - c)
+    ahead = device((z + 1 - 2 * c + NZ) % NZ, x, y, c)
+    behind = device((z + 2 * c - 1 + NZ) % NZ, x, y, c)
+
+    def piece(step):
+        return (z + (2 * c - 1) * step + 2 * NZ) % NZ
+
+    def passing(index, which, at):
+        slot = experts_ref.at[which, at]
+        return remote(slot, slot, ring_s.at[index], ring_r.at[index], ahead)
+
+    def crossing(index, which, at):
+        slot = experts_ref.at[which, at]
+        return remote(slot, slot, swap_s.at[index], swap_r.at[index], partner)
+
+    return partner, ahead, behind, piece, passing, crossing
+
+
+FIRST = 8
+
+
+def finish_ring(experts, after):
+    last = NZ // 2
+    chunks = 2 * (last - 1)
+
+    def kernel(after_ref, old_ref, experts_ref, ring_s, ring_r, swap_s, swap_r):
+        c = lax.axis_index("exp") % NC
+        partner, ahead, behind, piece, passing, crossing = column_ring(
+            experts_ref, ring_s, ring_r, swap_s, swap_r
+        )
+        greet([partner, ahead, behind])
+        for which in range(2):
+            passing(which, which, piece(FIRST // 2)).start()
+        for n in range(FIRST, chunks):
+            which, at = n % 2, piece(n // 2 + 1)
+            passing(n - FIRST, which, at).wait_recv()
+            if n + 2 < chunks:
+                passing(n + 2 - FIRST, which, at).start()
+            crossing(n - FIRST, which, at).start()
+        passing(chunks - FIRST, c, piece(last - 1)).start()
+        passing(chunks - FIRST, c, piece(last)).wait_recv()
+        crossing(chunks - FIRST, c, piece(last)).start()
+        for n in range(FIRST, chunks):
+            which, at = n % 2, piece(n // 2 + 1)
+            passing(n - FIRST, which, at).wait_send()
+            crossing(n - FIRST, which, at).wait()
+        passing(chunks - FIRST, c, piece(last)).wait_send()
+        crossing(chunks - FIRST, c, piece(last)).wait()
+
+    anywhere = pl.BlockSpec(memory_space=pl.ANY)
+    count = chunks + 1 - FIRST
+    moved = experts.size // 2
+    return pl.pallas_call(
+        kernel,
+        in_specs=[anywhere, anywhere],
+        out_specs=anywhere,
+        out_shape=jax.ShapeDtypeStruct(experts.shape, experts.dtype),
+        input_output_aliases={1: 0},
+        scratch_shapes=[pltpu.SemaphoreType.DMA((count,))] * 4,
+        compiler_params=pltpu.CompilerParams(
+            collective_id=1, has_side_effects=True, vmem_limit_bytes=8 * 2**20
+        ),
+        cost_estimate=pl.CostEstimate(
+            flops=0, bytes_accessed=20 * moved, transcendentals=0
+        ),
+        name="finish_ring",
+    )(after, experts)
+
+
 def fetch_and_attend(queries, keys, values, segment_ids, out_proj, expert_up, expert_down):
     shard_len, width = queries.shape
     block_rows = min(256, shard_len)
@@ -24,53 +120,31 @@
     scale = HEAD ** (-0.5) * math.log2(math.e)
     units, features = expert_up.shape[1:]
     rows = out_proj.shape[0] // PLANE
-    last = NZ // 2
 
     def kernel(
         q_ref, k_ref, v_ref, mq_ref, seg_ref, proj_ref, up_ref, down_ref,
         att_ref, whole_ref, experts_ref,
-        k2, v2, m2, ring_s, ring_r, swap_s, swap_r, send_s, recv_s, local_s,
+        k2, v2, m2, relay, ring_s, ring_r, swap_s, swap_r, send_s, recv_s, local_s,
+        spread_s, spread_r, rise_s, rise_r, gather_s, gather_r,
     ):
         ctx, exp = lax.axis_index("ctx"), lax.axis_index("exp")
         zh, x, y = ctx // PLANE, (ctx // NY) % NX, ctx % NY
         zl, c = exp // NC, exp % NC
         z, p = zh * ZL + zl, ctx % PLANE
 
-        def device(z, x, y, c):
-            return ((z // ZL) * PLANE + x * NY + y, (z % ZL) * NC + c)
-
-        def piece(step):
-            return (z + (2 * c - 1) * step + 2 * NZ) % NZ
-
-        partner = device(z, x, y, 1 - c)
-        ahead = device((z + 1 - 2 * c + NZ) % NZ, x, y, c)
-        behind = device((z + 2 * c - 1 + NZ) % NZ, x, y, c)
+        partner, ahead, behind, piece, ring_at, swap_at = column_ring(
+            experts_ref, ring_s, ring_r, swap_s, swap_r
+        )
         line = [device(zh * ZL + (zl + d) % ZL, x, y, c) for d in (1, 2, 3)]
         column = [device(z, x, (y + d) % NY, c) for d in (1, 2, 3)]
         right, left = device(z, (x + 1) % NX, y, c), device(z, (x + 3) % NX, y, c)
         after, before = ((ctx + 1) % N_CTX, exp), ((ctx + N_CTX - 1) % N_CTX, exp)
-        greeted = [partner, ahead, behind, *line, *column, right, left, after, before]
-        barrier = pltpu.get_barrier_semaphore()
-        for other in greeted:
-            pl.semaphore_signal(barrier, inc=1, device_id=other, device_id_type=MESH)
-        pl.semaphore_wait(barrier, len(greeted))
-
-        def remote(src, dst, sent, received, target):
-            return pltpu.make_async_remote_copy(
-                src_ref=src, dst_ref=dst, send_sem=sent, recv_sem=received,
-                device_id=target, device_id_type=MESH,
-            )
+        above, below = device((z + ZL) % NZ, x, y, c), device((z + NZ - ZL) % NZ, x, y, c)
+        mates = [(zh * PLANE + (p + d) % PLANE, exp) for d in range(1, PLANE)]
+        greet([partner, ahead, behind, *line, after, before, above, below, *mates])
 
         def other(src, dst, index, target):
             return remote(src, dst, send_s.at[index], recv_s.at[index], target)
-
-        def ring_at(index, which, at):
-            slot = experts_ref.at[which, at]
-            return remote(slot, slot, ring_s.at[index], ring_r.at[index], ahead)
-
-        def swap_at(index, which, at):
-            slot = experts_ref.at[which, at]
-            return remote(slot, slot, swap_s.at[index], swap_r.at[index], partner)
 
         locals_ = []
         pairs = []
@@ -82,11 +156,27 @@
             copy.start()
         early = pl.ds(0, shard_len)
         late = pl.ds(shard_len, shard_len)
-        shift = [
-            other(k_ref, k2.at[early], 2, after),
-            other(v_ref, v2.at[early], 3, after),
-            other(seg_ref, m2.at[:, early], 4, after),
-        ]
+        marks = other(seg_ref, m2.at[:, early], 4, after)
+        shift = [other(k_ref, k2.at[early], 2, after), other(v_ref, v2.at[early], 3, after)]
+        inside, final = p < PLANE - 1, p == PLANE - 1
+        part = shard_len // PLANE
+        both = ((k_ref, k2), (v_ref, v2))
+
+        def spread(kv, to):
+            return remote(
+                both[kv][0].at[pl.ds(to * part, part)], relay.at[0, kv],
+                spread_s.at[kv, to], spread_r.at[kv], (zh * PLANE + to, exp),
+            )
+
+        def rise(kv, src):
+            return remote(src, relay.at[1, kv], rise_s.at[kv], rise_r.at[kv], above)
+
+        def gather(kv, sender):
+            rows_there = both[kv][1].at[pl.ds(sender * part, part)]
+            return remote(
+                relay.at[1, kv], rows_there,
+                gather_s.at[kv], gather_r.at[kv, sender], (zh * PLANE, exp),
+            )
         stay = [
             pltpu.make_async_copy(k_ref, k2.at[late], local_s.at[2]),
             pltpu.make_async_copy(v_ref, v2.at[late], local_s.at[3]),
@@ -95,8 +185,21 @@
         rows_own = whole_ref.at[zl, c, p]
         proj_own = pltpu.make_async_copy(proj_ref.at[p], rows_own, local_s.at[5])
         along_z = [other(proj_ref.at[p], rows_own, 5 + d, line[d]) for d in range(3)]
-        for copy in along_z + shift + stay + [proj_own]:
+        for copy in along_z + stay + [marks, proj_own]:
             copy.start()
+
+        @pl.when(inside)
+        def _():
+            for copy in shift:
+                copy.start()
+
+        @pl.when(final)
+        def _():
+            for kv in range(2):
+                for to in range(PLANE - 1):
+                    spread(kv, to).start()
+                rise(kv, both[kv][0].at[pl.ds((PLANE - 1) * part, part)]).start()
+
         for copy in pairs:
             copy.wait()
         for copy in locals_:
@@ -145,16 +248,56 @@
         for copy in along_x:
             copy.start()
         forward(1, 1, 1)
+
+        @pl.when(inside)
+        def _():
+            for kv in range(2):
+                spread(kv, 0).wait_recv()
+                rise(kv, relay.at[0, kv]).start()
+
         forward(2, 2, 0)
         forward(3, 2, 1)
-        for copy in stay:
-            copy.wait()
-        for copy in shift:
-            copy.wait_recv()
+        for kv in range(2):
+            rise(kv, relay.at[0, kv]).wait_recv()
+        to_front = [
+            pltpu.make_async_copy(
+                relay.at[1, kv], both[kv][1].at[pl.ds(0, part)], local_s.at[6 + kv]
+            )
+            for kv in range(2)
+        ]
+
+        @pl.when(p > 0)
+        def _():
+            for kv in range(2):
+                gather(kv, p).start()
+
+        @pl.when(p == 0)
+        def _():
+            for copy in to_front:
+                copy.start()
+
+        forward(4, 3, 0)
         for copy in along_x:
             copy.wait_recv()
         for copy in opposite:
             copy.start()
+        forward(5, 3, 1)
+        for copy in stay:
+            copy.wait()
+        marks.wait_recv()
+
+        @pl.when(p > 0)
+        def _():
+            for copy in shift:
+                copy.wait_recv()
+
+        @pl.when(p == 0)
+        def _():
+            for kv in range(2):
+                to_front[kv].wait()
+                for sender in range(1, PLANE):
+                    gather(kv, sender).wait_recv()
+
         column_at = lax.broadcasted_iota(jnp.int32, (block_rows, span), 1)
         row_at = lax.broadcasted_iota(jnp.int32, (block_rows, span), 0)
 
@@ -179,36 +322,46 @@
             )
             att_ref[here, head] = (mixed / total).astype(att_ref.dtype)
 
-        per_turn = tiles * (width // HEAD) // 4
+        per_turn = tiles * (width // HEAD) // 2
 
         def turn(n, carry):
-            forward(n, n // 2 + 1, n % 2)
+            service(n, n // 2 + 1, n % 2)
 
             def inner(i, carry):
-                one_tile((n - 4) * per_turn + i)
+                one_tile((n - 6) * per_turn + i)
                 return carry
 
             return lax.fori_loop(0, per_turn, inner, carry)
 
-        lax.fori_loop(4, 8, turn, 0)
         for copy in opposite:
             copy.wait_recv()
         crossing.start()
-        for n in range(8, 12):
-            forward(n, n // 2 + 1, n % 2)
-        for which in range(2):
-            service(12 + which, last - 1, which)
-        ring_at(14, c, piece(last - 1)).start()
-        service(14, last, c)
-        for copy in along_z + along_y + along_x + opposite + shift:
+        lax.fori_loop(6, FIRST, turn, 0)
+        for copy in along_z + along_y + along_x + opposite + [marks]:
             copy.wait_send()
         crossing.wait()
-        for n in range(14):
-            at = z
-            ring_at(n, n % 2, at).wait_send()
-            swap_at(n, n % 2, at).wait()
-        ring_at(14, c, z).wait_send()
-        swap_at(14, c, z).wait()
+
+        @pl.when(inside)
+        def _():
+            for kv in range(2):
+                shift[kv].wait_send()
+                rise(kv, relay.at[0, kv]).wait_send()
+
+        @pl.when(final)
+        def _():
+            for kv in range(2):
+                for to in range(PLANE - 1):
+                    spread(kv, to).wait_send()
+                rise(kv, both[kv][0].at[pl.ds((PLANE - 1) * part, part)]).wait_send()
+
+        @pl.when(p > 0)
+        def _():
+            for kv in range(2):
+                gather(kv, p).wait_send()
+
+        for n in range(FIRST):
+            ring_at(n, n % 2, z).wait_send()
+            swap_at(n, n % 2, z).wait()
 
     anywhere = pl.BlockSpec(memory_space=pl.ANY)
     vmem = pl.BlockSpec(memory_space=pltpu.VMEM)
@@ -225,13 +378,20 @@
             pltpu.VMEM((2 * shard_len, width), keys.dtype),
             pltpu.VMEM((2 * shard_len, width), values.dtype),
             pltpu.VMEM((1, 2 * shard_len), jnp.int32),
-            pltpu.SemaphoreType.DMA((15,)),
-            pltpu.SemaphoreType.DMA((15,)),
-            pltpu.SemaphoreType.DMA((15,)),
-            pltpu.SemaphoreType.DMA((15,)),
+            pltpu.VMEM((2, 2, shard_len // PLANE, width), keys.dtype),
+            pltpu.SemaphoreType.DMA((FIRST,)),
+            pltpu.SemaphoreType.DMA((FIRST,)),
+            pltpu.SemaphoreType.DMA((FIRST,)),
+            pltpu.SemaphoreType.DMA((FIRST,)),
             pltpu.SemaphoreType.DMA((16,)),
             pltpu.SemaphoreType.DMA((16,)),
-            pltpu.SemaphoreType.DMA((6,)),
+            pltpu.SemaphoreType.DMA((8,)),
+            pltpu.SemaphoreType.DMA((2, PLANE)),
+            pltpu.SemaphoreType.DMA((2,)),
+            pltpu.SemaphoreType.DMA((2,)),
+            pltpu.SemaphoreType.DMA((2,)),
+            pltpu.SemaphoreType.DMA((2,)),
+            pltpu.SemaphoreType.DMA((2, PLANE)),
         ],
         compiler_params=pltpu.CompilerParams(
             collective_id=0, has_side_effects=True, vmem_limit_bytes=40 * 2**20
@@ -332,6 +492,7 @@
         axis_index_groups=plane_groups,
         tiled=True,
     )
+    experts_here = finish_ring(experts_here, outgoing)
     result = run_experts(arrived.reshape(PLANE, ZH, CAP, feature_count), experts_here)
     returned = lax.all_to_all(
         result.reshape(PLANE, ZH * CAP, feature_count),

time: 315 us -> 243 us (0.77)
  blocking collectives: 60.8 us -> 0 us
  Pallas kernels: 180 us -> 141 us
  local copies, waits for them, and re-layouts: 10.8 us -> 23.3 us
  starting transfers between devices: 7.93 us -> 18.5 us
  waiting for transfers between devices: 40.5 us -> 44.7 us
    pallas_call x1, Pallas kernels: 169 us -> 84.7 us  [fetch_and_attend(): pl.pallas_call(kernel, in_specs=[vmem, anywhere, anywhere, vmem, vmem, an...]
    all_to_all x1 -> x0, blocking collectives: 60.8 us -> none  [shards(): lax.all_to_all(outgoing.reshape(PLANE, ZH * CAP, feature_count), 'ctx', 0...]
    pallas_call x0 -> x1, Pallas kernels: none -> 46.5 us  [finish_ring(): pl.pallas_call(kernel, in_specs=[anywhere, anywhere], out_specs=anywhere,...]
    unnamed x27 -> x33, local copies, waits for them, and re-layouts: 9.15 us -> 21.6 us
    all_to_all x0 -> x1, starting transfers between devices: none -> 6.07 us  [shards(): lax.all_to_all(outgoing.reshape(PLANE, ZH * CAP, feature_count), 'ctx', 0...]
    all_to_all x1, waiting for transfers between devices: 29.6 us -> 33.7 us  [shards(): lax.all_to_all(result.reshape(PLANE, ZH * CAP, feature_count), 'ctx', 0,...]
    all_to_all x1, starting transfers between devices: 3.86 us -> 7.07 us  [shards(): lax.all_to_all(result.reshape(PLANE, ZH * CAP, feature_count), 'ctx', 0,...]
  transfers between devices with their start and end apart: 2 -> 3, of which waited for: 2 -> 2; matrix products, arithmetic and copies ran while one was open for 1% -> 2% of each run, Pallas kernels for 0% -> 19%
where the time goes in v3:
time: 243 us; the launch traced here: 241 us
  Pallas kernels  141 us (58%)
  waiting for transfers between devices  44.7 us (18%)
  local copies, waits for them, and re-layouts  23.3 us (10%)
  starting transfers between devices  18.5 us (8%)
  matrix products  8.77 us (4%)
  other arithmetic  3.77 us (2%)
    pallas_call x1, Pallas kernels, fetch_and_attend(): pl.pallas_call(kernel, in_specs=[vmem, anywhere, anywhere, vmem, vmem, an...  84.7 us
    pallas_call x1, Pallas kernels, finish_ring(): pl.pallas_call(kernel, in_specs=[anywhere, anywhere], out_specs=anywhere,...  46.5 us
    all_to_all x1, waiting for transfers between devices, shards(): lax.all_to_all(result.reshape(PLANE, ZH * CAP, feature_count), 'ctx', 0,...  33.7 us
    unnamed x33, local copies, waits for them, and re-layouts  21.6 us
    all_to_all x1, waiting for transfers between devices, shards(): lax.all_to_all(attention.reshape(groups, tok_rows, heads_here * HEAD), 'e...  10.9 us
    pallas_call x1, Pallas kernels, run_experts(): pl.pallas_call(kernel, grid=(count,), in_specs=[pl.BlockSpec(block, lambd...  10.3 us
    all_to_all x1, starting transfers between devices, shards(): lax.all_to_all(result.reshape(PLANE, ZH * CAP, feature_count), 'ctx', 0,...  7.07 us
    all_to_all x1, starting transfers between devices, shards(): lax.all_to_all(outgoing.reshape(PLANE, ZH * CAP, feature_count), 'ctx', 0...  6.07 us
  transfers between devices with their start and end apart: 3, of which 2 were waited for; matrix products, arithmetic and copies ran while one was open for 2% of the time, Pallas kernels for 19%

profile of v3, /device:TPU:1, one launch (start us, length us, event | category | flops | bytes accessed | tf_op | source)
XLA Modules:
  0.0 240.6 jit_solution(11416936136343437731)
XLA Ops:
  0.0 0.0 copy-start.15
  0.0 0.0 copy-start.12
  0.0 0.9 copy.24.mq_ref
  1.0 0.0 copy-start.3
  1.0 1.1 copy-done.3
  2.1 0.0 copy-start.4
  2.1 1.0 copy-done.4
  3.1 1.0 copy-done.5
  4.1 1.0 copy-done.6
  5.2 0.9 copy-done.7
  6.1 0.9 copy-done.8
  7.1 0.7 copy-done.9
  7.8 84.7 %fetch_and_attend.1 = (bf16[1024,256]{1,0:T(8,128)(2,1)}, bf16[4,2,16,16,1280]{4,3,2,1,0:T(8,128)(2,1)S(1)}, bf16[2,16,2,96,1280]{4,3,2,1,0:T(8,128)(2,1)}) custom-call(bf16[1024,256]{1,0:T(8,128)(2,1)S(1)} %copy-done.4, bf16[1024,256]{1,0:T(8,128)(2,1)S(1)} %copy-done.5, bf16[1024,256]{1,0:T(8,128)(2,1)S(1)} %copy-done.6, s32[1024,1]{1,0:T(8,128)S(1)} %copy.24.mq_ref, ...), custom_call_target="tpu_custom_call" | custom-call | tf_op jit(solution)/shard_map/fetch_and_attend/pallas_call | solution.py:368
  92.5 0.0 copy-start.2
  92.5 2.2 copy-done.2
  94.7 5.3 %all-to-all-start = ((bf16[8,128,256]{2,1,0:T(8,128)(2,1)}), bf16[8,128,256]{2,1,0:T(8,128)(2,1)S(1)}, u32[]{:S(2)}, u32[]{:S(2)}) async-start(bf16[8,128,256]{2,1,0:T(8,128)(2,1)} %bitcast.3), calls=%async_computation | async-start | bytes 1048576 | tf_op jit(solution)/shard_map/all_to_all | solution.py:456
  100.1 0.0 copy-done.15
  100.1 0.1 copy.25
  100.2 0.1 eq.44
  100.3 0.1 eq.40
  100.5 1.8 reduce-window.6
  102.3 0.3 slice_reduce_fusion
  102.6 0.1 fusion.10
  102.7 0.1 reduce_sum.30
  102.9 0.1 fusion.18
  102.9 0.1 copy.32
  103.0 0.5 fusion
  103.5 10.9 %all-to-all-done = bf16[8,128,256]{2,1,0:T(8,128)(2,1)S(1)} async-done(((bf16[8,128,256]{2,1,0:T(8,128)(2,1)}), bf16[8,128,256]{2,1,0:T(8,128)(2,1)S(1)}, u32[]{:S(2)}, u32[]{:S(2)}) %all-to-all-start) | async-done | bytes 524320 | tf_op jit(solution)/shard_map/all_to_all | solution.py:456
  114.4 0.0 copy-done.12
  114.5 3.4 %multiply_reduce_fusion = (f32[128]{0:T(128)S(1)}, f32[128,1280]{1,0:T(8,128)S(1)}) fusion(bf16[8,128,256]{2,1,0:T(8,128)(2,1)S(1)} %all-to-all-done, bf16[8,256,1280]{2,1,0:T(8,128)(2,1)} %bitcast.42, bf16[128,1280]{1,0:T(8,128)(2,1)S(1)} %copy-done.12), kind=kOutput, calls=%fused_computation.12 | convolution fusion | flops 672071552 | bytes 6750720 | tf_op jit(solution)/shard_map/etk,ekd->td/dot_general | solution.py:459
  117.9 0.0 copy-done.13
  117.9 2.4 %convolution_convert_fusion.after_ref = bf16[1024,1280]{1,0:T(8,128)(2,1)} fusion(pred[128,1024]{1,0:T(8,128)(4,1)S(1)} %fusion, f32[128,1280]{1,0:T(8,128)S(1)} %get-tuple-element.12, f32[1280]{0:T(1024)S(1)} %copy-done.13, f32[128]{0:T(128)S(1)} %add_rsqrt_fusion), kind=kOutput, calls=%fused_computation | convolution fusion | flops 337346560 | bytes 3413504 | tf_op jit(solution)/shard_map/dot_general | solution.py:483
  120.3 6.1 %all-to-all-start.1 = ((bf16[16,64,1280]{2,1,0:T(8,128)(2,1)}), bf16[16,64,1280]{2,1,0:T(8,128)(2,1)S(1)}, u32[]{:S(2)}, u32[]{:S(2)}) async-start(bf16[16,64,1280]{2,1,0:T(8,128)(2,1)} %bitcast.7), calls=%async_computation.1 | async-start | bytes 5242880 | tf_op jit(solution)/shard_map/all_to_all | solution.py:487
  126.4 0.0 copy-start
  126.4 5.5 %copy-done = bf16[2,16,2,96,1280]{4,3,2,1,0:T(8,128)(2,1)S(1)} copy-done((bf16[2,16,2,96,1280]{4,3,2,1,0:T(8,128)(2,1)S(1)}, bf16[2,16,2,96,1280]{4,3,2,1,0:T(8,128)(2,1)}, u32[]{:S(2)}) %copy-start) | copy-done | bytes 15728664
  131.9 46.5 %finish_ring.1.up_ref.down_ref = bf16[2,16,2,96,1280]{4,3,2,1,0:T(8,128)(2,1)S(1)} custom-call(bf16[1024,1280]{1,0:T(8,128)(2,1)} %convolution_convert_fusion.after_ref, bf16[2,16,2,96,1280]{4,3,2,1,0:T(8,128)(2,1)S(1)} %copy-done), custom_call_target="tpu_custom_call", output_to_operand_aliasing={{}: (1, {})} | custom-call | bytes 78643200 | tf_op jit(solution)/shard_map/finish_ring/pallas_call | solution.py:98
  178.4 0.0 copy-start.1
  178.4 5.5 %copy-done.1 = bf16[2,16,2,96,1280]{4,3,2,1,0:T(8,128)(2,1)} copy-done((bf16[2,16,2,96,1280]{4,3,2,1,0:T(8,128)(2,1)}, bf16[2,16,2,96,1280]{4,3,2,1,0:T(8,128)(2,1)S(1)}, u32[]{:S(2)}) %copy-start.1) | copy-done | bytes 15728664
  183.9 0.0 all-to-all-done.1
  183.9 1.5 copy-done.10
  185.3 10.3 %run_experts.1 = bf16[16,4,16,1280]{3,2,1,0:T(8,128)(2,1)} custom-call(bf16[16,4,16,1280]{3,2,1,0:T(8,128)(2,1)} %bitcast.48, bf16[2,16,2,96,1280]{4,3,2,1,0:T(8,128)(2,1)} %copy-done.1, bf16[2,16,2,96,1280]{4,3,2,1,0:T(8,128)(2,1)} %copy-done.1), custom_call_target="tpu_custom_call" | custom-call | tf_op jit(solution)/shard_map/run_experts/pallas_call | solution.py:422
  195.6 7.1 %all-to-all-start.2 = ((bf16[16,64,1280]{2,1,0:T(8,128)(2,1)}), bf16[16,64,1280]{2,1,0:T(8,128)(2,1)S(1)}, u32[]{:S(2)}, u32[]{:S(2)}) async-start(bf16[16,64,1280]{2,1,0:T(8,128)(2,1)} %bitcast.49), calls=%async_computation.2 | async-start | bytes 5242880 | tf_op jit(solution)/shard_map/all_to_all | solution.py:497
  202.7 0.0 copy-done.14
  202.7 1.2 select_reduce_fusion
  203.9 33.7 %all-to-all-done.2 = bf16[16,64,1280]{2,1,0:T(8,128)(2,1)S(1)} async-done(((bf16[16,64,1280]{2,1,0:T(8,128)(2,1)}), bf16[16,64,1280]{2,1,0:T(8,128)(2,1)S(1)}, u32[]{:S(2)}, u32[]{:S(2)}) %all-to-all-start.2) | async-done | bytes 2621472 | tf_op jit(solution)/shard_map/all_to_all | solution.py:497
  237.6 1.6 fusion.13
  239.3 0.0 copy-done.11
  239.3 1.3 fusion.3
  (12 shorter events, 0.1 us)
Async XLA Ops:
  0.0 100.1 %copy-start.15 = (s32[128,6]{0,1:T(8,128)S(1)}, s32[128,6]{0,1:T(8,128)}, u32[]{:S(2)}) copy-start(s32[128,6]{0,1:T(8,128)} %param.18) | copy-start | bytes 9220
  0.0 114.4 %copy-start.12 = (bf16[128,1280]{1,0:T(8,128)(2,1)S(1)}, bf16[128,1280]{1,0:T(8,128)(2,1)}, u32[]{:S(2)}) copy-start(bf16[128,1280]{1,0:T(8,128)(2,1)} %param.16) | copy-start | bytes 983044
  1.0 1.1 copy-start.3
  2.1 1.0 copy-start.4
  3.1 1.0 copy-start.5
  4.1 1.0 copy-start.6
  5.2 0.9 copy-start.7
  6.1 0.9 copy-start.8
  7.1 0.7 copy-start.9
  92.5 2.3 copy-start.2
  94.7 19.7 %all-to-all-start = ((bf16[8,128,256]{2,1,0:T(8,128)(2,1)}), bf16[8,128,256]{2,1,0:T(8,128)(2,1)S(1)}, u32[]{:S(2)}, u32[]{:S(2)}) async-start(bf16[8,128,256]{2,1,0:T(8,128)(2,1)} %bitcast.3), calls=%async_computation | async-start | bytes 1048576 | tf_op jit(solution)/shard_map/all_to_all | solution.py:456
  114.4 3.5 %copy-start.13 = (f32[1280]{0:T(1024)S(1)}, f32[1280]{0:T(1024)}, u32[]{:S(2)}) copy-start(f32[1280]{0:T(1024)} %param.17) | copy-start | bytes 15364
  120.3 63.6 %all-to-all-start.1 = ((bf16[16,64,1280]{2,1,0:T(8,128)(2,1)}), bf16[16,64,1280]{2,1,0:T(8,128)(2,1)S(1)}, u32[]{:S(2)}, u32[]{:S(2)}) async-start(bf16[16,64,1280]{2,1,0:T(8,128)(2,1)} %bitcast.7), calls=%async_computation.1 | async-start | bytes 5242880 | tf_op jit(solution)/shard_map/all_to_all | solution.py:487
  126.4 5.5 %copy-start = (bf16[2,16,2,96,1280]{4,3,2,1,0:T(8,128)(2,1)S(1)}, bf16[2,16,2,96,1280]{4,3,2,1,0:T(8,128)(2,1)}, u32[]{:S(2)}) copy-start(bf16[2,16,2,96,1280]{4,3,2,1,0:T(8,128)(2,1)} %get-tuple-element.10.old_ref) | copy-start | bytes 47185924
  178.4 5.5 %copy-start.1 = (bf16[2,16,2,96,1280]{4,3,2,1,0:T(8,128)(2,1)}, bf16[2,16,2,96,1280]{4,3,2,1,0:T(8,128)(2,1)S(1)}, u32[]{:S(2)}) copy-start(bf16[2,16,2,96,1280]{4,3,2,1,0:T(8,128)(2,1)S(1)} %finish_ring.1.up_ref.down_ref) | copy-start | bytes 47185924
  183.9 1.5 copy-start.10
  195.6 7.1 %copy-start.14 = (f32[128,6]{0,1:T(8,128)S(1)}, f32[128,6]{0,1:T(8,128)}, u32[]{:S(2)}) copy-start(f32[128,6]{0,1:T(8,128)} %param.19) | copy-start | bytes 9220
  195.6 42.0 %all-to-all-start.2 = ((bf16[16,64,1280]{2,1,0:T(8,128)(2,1)}), bf16[16,64,1280]{2,1,0:T(8,128)(2,1)S(1)}, u32[]{:S(2)}, u32[]{:S(2)}) async-start(bf16[16,64,1280]{2,1,0:T(8,128)(2,1)} %bitcast.49), calls=%async_computation.2 | async-start | bytes 5242880 | tf_op jit(solution)/shard_map/all_to_all | solution.py:497
  237.6 1.6 copy-start.11

commit v4 on v3

--- a/solution.py
+++ b/solution.py
@@ -61,7 +61,7 @@
     return partner, ahead, behind, piece, passing, crossing
 
 
-FIRST = 8
+FIRST = 10
 
 
 def finish_ring(experts, after):
@@ -103,7 +103,7 @@
         input_output_aliases={1: 0},
         scratch_shapes=[pltpu.SemaphoreType.DMA((count,))] * 4,
         compiler_params=pltpu.CompilerParams(
-            collective_id=1, has_side_effects=True, vmem_limit_bytes=8 * 2**20
+            collective_id=1, has_side_effects=True, vmem_limit_bytes=60 * 2**20
         ),
         cost_estimate=pl.CostEstimate(
             flops=0, bytes_accessed=20 * moved, transcendentals=0
@@ -234,8 +234,9 @@
             other(from_left, from_left, 13, right),
             other(from_right, from_right, 14, left),
         ]
-        core_half = whole_ref.at[:, c]
-        crossing = other(core_half, core_half, 15, partner)
+        crossing = [
+            other(x_block((x + d) % NX), x_block((x + d) % NX), 15 + d, partner) for d in range(NX)
+        ]
 
         for copy in along_z:
             copy.wait_recv()
@@ -245,7 +246,7 @@
         forward(0, 1, 0)
         for copy in along_y:
             copy.wait_recv()
-        for copy in along_x:
+        for copy in along_x + crossing[:1]:
             copy.start()
         forward(1, 1, 1)
 
@@ -279,9 +280,10 @@
         forward(4, 3, 0)
         for copy in along_x:
             copy.wait_recv()
-        for copy in opposite:
+        for copy in opposite + [crossing[1], crossing[3]]:
             copy.start()
-        forward(5, 3, 1)
+        for n in range(5, FIRST - 2):
+            forward(n, n // 2 + 1, n % 2)
         for copy in stay:
             copy.wait()
         marks.wait_recv()
@@ -328,18 +330,19 @@
             service(n, n // 2 + 1, n % 2)
 
             def inner(i, carry):
-                one_tile((n - 6) * per_turn + i)
+                one_tile((n - FIRST + 2) * per_turn + i)
                 return carry
 
             return lax.fori_loop(0, per_turn, inner, carry)
 
+        lax.fori_loop(FIRST - 2, FIRST, turn, 0)
         for copy in opposite:
             copy.wait_recv()
-        crossing.start()
-        lax.fori_loop(6, FIRST, turn, 0)
+        crossing[2].start()
         for copy in along_z + along_y + along_x + opposite + [marks]:
             copy.wait_send()
-        crossing.wait()
+        for copy in crossing:
+            copy.wait()
 
         @pl.when(inside)
         def _():
@@ -383,8 +386,8 @@
             pltpu.SemaphoreType.DMA((FIRST,)),
             pltpu.SemaphoreType.DMA((FIRST,)),
             pltpu.SemaphoreType.DMA((FIRST,)),
-            pltpu.SemaphoreType.DMA((16,)),
-            pltpu.SemaphoreType.DMA((16,)),
+            pltpu.SemaphoreType.DMA((19,)),
+            pltpu.SemaphoreType.DMA((19,)),
             pltpu.SemaphoreType.DMA((8,)),
             pltpu.SemaphoreType.DMA((2, PLANE)),
             pltpu.SemaphoreType.DMA((2,)),

time: 243 us -> 234 us (0.963)
  local copies, waits for them, and re-layouts: 23.3 us -> 12.3 us
  Pallas kernels: 141 us -> 146 us
    pallas_call x1, Pallas kernels: 84.7 us -> 98.9 us  [fetch_and_attend(): pl.pallas_call(kernel, in_specs=[vmem, anywhere, anywhere, vmem, vmem, an...]
    unnamed x33 -> x29, local copies, waits for them, and re-layouts: 21.6 us -> 10.6 us
    pallas_call x1, Pallas kernels: 46.5 us -> 36.9 us  [finish_ring(): pl.pallas_call(kernel, in_specs=[anywhere, anywhere], out_specs=anywhere,...]
  transfers between devices with their start and end apart: 3 -> 3, of which waited for: 2 -> 2; matrix products, arithmetic and copies ran while one was open for 2% -> 2% of each run, Pallas kernels for 19% -> 16%
where the time goes in v4:
time: 234 us; the launch traced here: 232 us
  Pallas kernels  146 us (62%)
  waiting for transfers between devices  44.7 us (19%)
  starting transfers between devices  16.7 us (7%)
  local copies, waits for them, and re-layouts  12.3 us (5%)
  matrix products  8.76 us (4%)
  other arithmetic  3.76 us (2%)
    pallas_call x1, Pallas kernels, fetch_and_attend(): pl.pallas_call(kernel, in_specs=[vmem, anywhere, anywhere, vmem, vmem, an...  98.9 us
    pallas_call x1, Pallas kernels, finish_ring(): pl.pallas_call(kernel, in_specs=[anywhere, anywhere], out_specs=anywhere,...  36.9 us
    all_to_all x1, waiting for transfers between devices, shards(): lax.all_to_all(result.reshape(PLANE, ZH * CAP, feature_count), 'ctx', 0,...  33.7 us
    all_to_all x1, waiting for transfers between devices, shards(): lax.all_to_all(attention.reshape(groups, tok_rows, heads_here * HEAD), 'e...  10.9 us
    unnamed x29, local copies, waits for them, and re-layouts  10.6 us
    pallas_call x1, Pallas kernels, run_experts(): pl.pallas_call(kernel, grid=(count,), in_specs=[pl.BlockSpec(block, lambd...  10.3 us
    all_to_all x1, starting transfers between devices, shards(): lax.all_to_all(result.reshape(PLANE, ZH * CAP, feature_count), 'ctx', 0,...  7.06 us
    all_to_all x1, starting transfers between devices, shards(): lax.all_to_all(outgoing.reshape(PLANE, ZH * CAP, feature_count), 'ctx', 0...  6.06 us
  transfers between devices with their start and end apart: 3, of which 2 were waited for; matrix products, arithmetic and copies ran while one was open for 2% of the time, Pallas kernels for 16%

profile of v4, /device:TPU:1, one launch (start us, length us, event | category | flops | bytes accessed | tf_op | source)
XLA Modules:
  0.0 232.3 jit_solution(5240992719144932792)
XLA Ops:
  0.0 0.0 copy-start.13
  0.0 0.0 copy-start.10
  0.0 0.9 copy.24.mq_ref
  1.0 0.0 copy-start.1
  1.0 1.1 copy-done.1
  2.1 0.0 copy-start.2
  2.1 1.0 copy-done.2
  3.1 1.0 copy-done.3
  4.1 0.0 copy-start.4
  4.1 1.0 copy-done.4
  5.2 0.0 copy-start.5
  5.2 0.9 copy-done.5
  6.1 0.0 copy-start.6
  6.1 0.9 copy-done.6
  7.1 0.7 copy-done.7
  7.8 98.9 %fetch_and_attend.1 = (bf16[1024,256]{1,0:T(8,128)(2,1)}, bf16[4,2,16,16,1280]{4,3,2,1,0:T(8,128)(2,1)S(1)}, bf16[2,16,2,96,1280]{4,3,2,1,0:T(8,128)(2,1)}) custom-call(bf16[1024,256]{1,0:T(8,128)(2,1)S(1)} %copy-done.2, bf16[1024,256]{1,0:T(8,128)(2,1)S(1)} %copy-done.3, bf16[1024,256]{1,0:T(8,128)(2,1)S(1)} %copy-done.4, s32[1024,1]{1,0:T(8,128)S(1)} %copy.24.mq_ref, ...), custom_call_target="tpu_custom_call" | custom-call | tf_op jit(solution)/shard_map/fetch_and_attend/pallas_call | solution.py:371
  106.6 0.0 copy-start
  106.6 2.2 copy-done
  108.9 3.5 %all-to-all-start = ((bf16[8,128,256]{2,1,0:T(8,128)(2,1)}), bf16[8,128,256]{2,1,0:T(8,128)(2,1)S(1)}, u32[]{:S(2)}, u32[]{:S(2)}) async-start(bf16[8,128,256]{2,1,0:T(8,128)(2,1)} %bitcast.3), calls=%async_computation | async-start | bytes 1048576 | tf_op jit(solution)/shard_map/all_to_all | solution.py:459
  112.4 0.0 copy-done.13
  112.4 0.1 copy.25
  112.5 0.1 eq.44
  112.7 0.1 eq.40
  112.8 1.8 reduce-window.6
  114.6 0.3 slice_reduce_fusion
  114.9 0.1 fusion.10
  115.1 0.1 reduce_sum.30
  115.2 0.1 fusion.18
  115.3 0.1 copy.32
  115.3 0.5 fusion
  115.9 10.9 %all-to-all-done = bf16[8,128,256]{2,1,0:T(8,128)(2,1)S(1)} async-done(((bf16[8,128,256]{2,1,0:T(8,128)(2,1)}), bf16[8,128,256]{2,1,0:T(8,128)(2,1)S(1)}, u32[]{:S(2)}, u32[]{:S(2)}) %all-to-all-start) | async-done | bytes 524320 | tf_op jit(solution)/shard_map/all_to_all | solution.py:459
  126.8 0.0 copy-done.10
  126.8 3.4 %multiply_reduce_fusion = (f32[128]{0:T(128)S(1)}, f32[128,1280]{1,0:T(8,128)S(1)}) fusion(bf16[8,128,256]{2,1,0:T(8,128)(2,1)S(1)} %all-to-all-done, bf16[8,256,1280]{2,1,0:T(8,128)(2,1)} %bitcast.42, bf16[128,1280]{1,0:T(8,128)(2,1)S(1)} %copy-done.10), kind=kOutput, calls=%fused_computation.12 | convolution fusion | flops 672071552 | bytes 6750720 | tf_op jit(solution)/shard_map/etk,ekd->td/dot_general | solution.py:462
  130.2 0.0 copy-done.11
  130.3 2.4 %convolution_convert_fusion.after_ref = bf16[1024,1280]{1,0:T(8,128)(2,1)} fusion(pred[128,1024]{1,0:T(8,128)(4,1)S(1)} %fusion, f32[128,1280]{1,0:T(8,128)S(1)} %get-tuple-element.12, f32[1280]{0:T(1024)S(1)} %copy-done.11, f32[128]{0:T(128)S(1)} %add_rsqrt_fusion), kind=kOutput, calls=%fused_computation | convolution fusion | flops 337346560 | bytes 3413504 | tf_op jit(solution)/shard_map/dot_general | solution.py:486
  132.7 6.1 %all-to-all-start.1 = ((bf16[16,64,1280]{2,1,0:T(8,128)(2,1)}), bf16[16,64,1280]{2,1,0:T(8,128)(2,1)S(1)}, u32[]{:S(2)}, u32[]{:S(2)}) async-start(bf16[16,64,1280]{2,1,0:T(8,128)(2,1)} %bitcast.7), calls=%async_computation.1 | async-start | bytes 5242880 | tf_op jit(solution)/shard_map/all_to_all | solution.py:490
  138.7 36.9 %finish_ring.1.up_ref.down_ref = bf16[2,16,2,96,1280]{4,3,2,1,0:T(8,128)(2,1)} custom-call(bf16[1024,1280]{1,0:T(8,128)(2,1)} %convolution_convert_fusion.after_ref, bf16[2,16,2,96,1280]{4,3,2,1,0:T(8,128)(2,1)} %get-tuple-element.10.old_ref), custom_call_target="tpu_custom_call", output_to_operand_aliasing={{}: (1, {})} | custom-call | bytes 78643200 | tf_op jit(solution)/shard_map/finish_ring/pallas_call | solution.py:98
  175.6 0.0 all-to-all-done.1
  175.6 0.0 copy-start.8
  175.6 1.4 copy-done.8
  177.1 10.3 %run_experts.1 = bf16[16,4,16,1280]{3,2,1,0:T(8,128)(2,1)} custom-call(bf16[16,4,16,1280]{3,2,1,0:T(8,128)(2,1)} %bitcast.48, bf16[2,16,2,96,1280]{4,3,2,1,0:T(8,128)(2,1)} %finish_ring.1.up_ref.down_ref, bf16[2,16,2,96,1280]{4,3,2,1,0:T(8,128)(2,1)} %finish_ring.1.up_ref.down_ref), custom_call_target="tpu_custom_call" | custom-call | tf_op jit(solution)/shard_map/run_experts/pallas_call | solution.py:425
  187.4 7.1 %all-to-all-start.2 = ((bf16[16,64,1280]{2,1,0:T(8,128)(2,1)}), bf16[16,64,1280]{2,1,0:T(8,128)(2,1)S(1)}, u32[]{:S(2)}, u32[]{:S(2)}) async-start(bf16[16,64,1280]{2,1,0:T(8,128)(2,1)} %bitcast.49), calls=%async_computation.2 | async-start | bytes 5242880 | tf_op jit(solution)/shard_map/all_to_all | solution.py:500
  194.4 0.0 copy-done.12
  194.4 1.2 select_reduce_fusion
  195.6 33.7 %all-to-all-done.2 = bf16[16,64,1280]{2,1,0:T(8,128)(2,1)S(1)} async-done(((bf16[16,64,1280]{2,1,0:T(8,128)(2,1)}), bf16[16,64,1280]{2,1,0:T(8,128)(2,1)S(1)}, u32[]{:S(2)}, u32[]{:S(2)}) %all-to-all-start.2) | async-done | bytes 2621472 | tf_op jit(solution)/shard_map/all_to_all | solution.py:500
  229.4 1.6 fusion.13
  231.0 0.0 copy-done.9
  231.0 1.3 fusion.3
  (8 shorter events, 0.1 us)
Async XLA Ops:
  0.0 112.4 %copy-start.13 = (s32[128,6]{0,1:T(8,128)S(1)}, s32[128,6]{0,1:T(8,128)}, u32[]{:S(2)}) copy-start(s32[128,6]{0,1:T(8,128)} %param.18) | copy-start | bytes 9220
  0.0 126.8 %copy-start.10 = (bf16[128,1280]{1,0:T(8,128)(2,1)S(1)}, bf16[128,1280]{1,0:T(8,128)(2,1)}, u32[]{:S(2)}) copy-start(bf16[128,1280]{1,0:T(8,128)(2,1)} %param.16) | copy-start | bytes 983044
  1.0 1.1 copy-start.1
  2.1 1.0 copy-start.2
  3.1 1.0 copy-start.3
  4.1 1.0 copy-start.4
  5.2 0.9 copy-start.5
  6.1 0.9 copy-start.6
  7.1 0.7 copy-start.7
  106.6 2.2 copy-start
  108.9 17.9 %all-to-all-start = ((bf16[8,128,256]{2,1,0:T(8,128)(2,1)}), bf16[8,128,256]{2,1,0:T(8,128)(2,1)S(1)}, u32[]{:S(2)}, u32[]{:S(2)}) async-start(bf16[8,128,256]{2,1,0:T(8,128)(2,1)} %bitcast.3), calls=%async_computation | async-start | bytes 1048576 | tf_op jit(solution)/shard_map/all_to_all | solution.py:459
  126.8 3.5 %copy-start.11 = (f32[1280]{0:T(1024)S(1)}, f32[1280]{0:T(1024)}, u32[]{:S(2)}) copy-start(f32[1280]{0:T(1024)} %param.17) | copy-start | bytes 15364
  132.7 43.0 %all-to-all-start.1 = ((bf16[16,64,1280]{2,1,0:T(8,128)(2,1)}), bf16[16,64,1280]{2,1,0:T(8,128)(2,1)S(1)}, u32[]{:S(2)}, u32[]{:S(2)}) async-start(bf16[16,64,1280]{2,1,0:T(8,128)(2,1)} %bitcast.7), calls=%async_computation.1 | async-start | bytes 5242880 | tf_op jit(solution)/shard_map/all_to_all | solution.py:490
  175.6 1.5 copy-start.8
  187.4 7.1 %copy-start.12 = (f32[128,6]{0,1:T(8,128)S(1)}, f32[128,6]{0,1:T(8,128)}, u32[]{:S(2)}) copy-start(f32[128,6]{0,1:T(8,128)} %param.19) | copy-start | bytes 9220
  187.4 42.0 %all-to-all-start.2 = ((bf16[16,64,1280]{2,1,0:T(8,128)(2,1)}), bf16[16,64,1280]{2,1,0:T(8,128)(2,1)S(1)}, u32[]{:S(2)}, u32[]{:S(2)}) async-start(bf16[16,64,1280]{2,1,0:T(8,128)(2,1)} %bitcast.49), calls=%async_computation.2 | async-start | bytes 5242880 | tf_op jit(solution)/shard_map/all_to_all | solution.py:500
  229.4 1.6 copy-start.9
